TPU v7x, 32 devices: a whole 2x2x4 slice. The times are simulated.
32 devices in a mesh: groups: 2 (over x), ctx: 16 (over z, y, core).
Axes of the slice: x: 2, y: 2, z: 4, core: 2. Of those that a mesh axis runs over, the one named last changes fastest.
Arguments:
- queries: bfloat16 [4096, 1024], P(('groups', 'ctx')), parts along dimension 0, may hold values from -27 to 27
- keys: bfloat16 [4096, 1024], P(('groups', 'ctx')), parts along dimension 0, may hold values from -6 to 6
- values: bfloat16 [4096, 1024], P(('groups', 'ctx')), parts along dimension 0, may hold values from -6 to 6
- resid: bfloat16 [4096, 2048], P(('groups', 'ctx')), parts along dimension 0, may hold values from -6 to 6
- out_proj: bfloat16 [1024, 2048], replicated, may hold values from -0.1875 to 0.1875
- norm_gain: float32 [2048], replicated, may hold values from 0.25 to 1.75
- up_proj: bfloat16 [2048, 4096], P(None, 'ctx'), may hold values from -0.125 to 0.125
- down_proj: bfloat16 [2048, 4096], P(None, 'ctx'), may hold values from -0.09375 to 0.09375
- router: bfloat16 [2048, 2], replicated, may hold values from -0.125 to 0.125
- expert_ids: int32 [4096, 1], P(('groups', 'ctx')), parts along dimension 0, may hold values from 0 to 1; in each aligned block of 128 rows (0 to 127, 128 to 255, ...) at most 80 rows name the same one
- expert_in: bfloat16 [16, 2048, 512], P('ctx'), may hold values from -0.125 to 0.125
- expert_out: bfloat16 [16, 512, 2048], P('ctx'), may hold values from -0.09375 to 0.09375
Outputs:
- layer_out: bfloat16 [4096, 2048], P(('groups', 'ctx')), parts along dimension 0
There are 2 independent parts, one for each index of `groups`. A program takes and returns all parts, laid end to end along the dimension named above; an argument that names none is the same for every part. Nothing has to cross between parts.
Inputs may be any that keep to these rules, and one draw needn't show every extreme that they name: `expert_ids`: among the 128 tokens of one index of ctx, at most 80 name the same expert; in every draw some index of ctx has 80 tokens naming one expert.
All inputs are finite; a program needn't handle non-finite values.
Results may differ from a plain program's by a relative error of at most 0.0075.
Values may be sent and summed in bfloat16 or wider, within the bound.
No kernel may reach another device: no remote copies, remote signals or barrier semaphores. Data moves between devices by JAX's collectives and lax.ppermute only.
A program may use at most 192 MiB of HBM per device.

v0:
```python
import functools
import jax
import jax.numpy as jnp
from jax import lax
from jax.experimental import pallas as pl
from jax.experimental.pallas import tpu as pltpu
from jax.sharding import PartitionSpec as P

DH = 128
SPLIT = 8


NEG_FILL = -1e30
EPSILON = 1e-06


def from_partner(array, axis, apart):
    return lax.ppermute(array, axis, [(i, i ^ 1 << apart) for i in range(lax.axis_size(axis))])


def update_state(state, query_rows, query_offset, key_block, value_block, key_offset):
    maxima, totals, numer = state
    count_query = query_rows.shape[0]
    count_keys = key_block.shape[0]
    head_count = query_rows.shape[1] // DH
    query_heads = query_rows.reshape(count_query, head_count, DH)
    key_heads = key_block.reshape(count_keys, head_count, DH)
    value_heads = value_block.reshape(count_keys, head_count, DH)
    scores = jnp.einsum(
        "qhd,khd->hqk", query_heads, key_heads, preferred_element_type=jnp.float32
    ) * DH ** (-0.5)
    query_positions = query_offset + jnp.arange(count_query, dtype=jnp.int32)
    key_positions = key_offset + jnp.arange(count_keys, dtype=jnp.int32)
    visible = (key_positions[None, :] <= query_positions[:, None])[None]
    masked = jnp.where(visible, scores, NEG_FILL)
    new_max = jnp.maximum(maxima, jnp.max(masked, axis=2))
    weights = jnp.where(visible, jnp.exp(masked - new_max[..., None]), 0.0)
    factor = jnp.exp(maxima - new_max)
    totals = totals * factor + jnp.sum(weights, axis=2)
    numer = numer * factor[..., None] + jnp.einsum(
        "hqk,khd->hqd",
        weights.astype(jnp.bfloat16),
        value_heads,
        preferred_element_type=jnp.float32,
    )
    return (new_max, totals, numer)


def attend(query_sets, keys, values):
    head_count = keys.shape[1] // DH
    initial = []
    for query_rows, query_offset in query_sets:
        count_query = query_rows.shape[0]
        initial.append(
            (
                jnp.full((head_count, count_query), NEG_FILL, jnp.float32),
                jnp.zeros((head_count, count_query), jnp.float32),
                jnp.zeros((head_count, count_query, DH), jnp.float32),
            )
        )
    states = tuple(initial)
    key_offset = jnp.int32(0)
    key_whole = lax.all_gather(keys, "ctx", axis=0, tiled=True)
    value_whole = lax.all_gather(values, "ctx", axis=0, tiled=True)
    total_keys = key_whole.shape[0]
    step_rows = min(total_keys, 1024)
    for begin in range(0, total_keys, step_rows):
        key_block = key_whole[begin : begin + step_rows]
        value_block = value_whole[begin : begin + step_rows]
        block_offset = key_offset + begin
        query_rows, query_offset = query_sets[0]
        needed = block_offset <= query_offset + query_rows.shape[0] - 1
        updated = [
            lax.cond(
                needed,
                lambda carried, rows_now=query_rows, offset_now=query_offset, keys_now=key_block, values_now=value_block, start_now=block_offset: update_state(
                    carried, rows_now, offset_now, keys_now, values_now, start_now
                ),
                lambda carried: carried,
                states[0],
            )
        ]
        states = tuple(updated)
    results = []
    for maxima, totals, numer in states:
        result = (numer / totals[..., None]).astype(jnp.bfloat16)
        results.append(
            jnp.transpose(result, (1, 0, 2)).reshape(result.shape[1], result.shape[0] * DH)
        )
    return results


def body(
    queries,
    keys,
    values,
    resid,
    out_proj,
    norm_gain,
    up_proj,
    down_proj,
    router,
    expert_ids,
    expert_in,
    expert_out,
):
    tok_rows = queries.shape[0]
    width = resid.shape[1]
    live_count = router.shape[1]
    ctx_count = lax.axis_size("ctx")
    device_index = lax.axis_index("ctx")
    base_offset = device_index * tok_rows
    attn = attend([(queries, base_offset)], keys, values)[0]
    mixed = resid.astype(jnp.float32) + jnp.dot(attn, out_proj, preferred_element_type=jnp.float32)
    normed = (
        mixed * lax.rsqrt(jnp.mean(mixed * mixed, axis=1, keepdims=True) + EPSILON) * norm_gain
    ).astype(jnp.bfloat16)
    mlp_blocks = jnp.stack([up_proj, down_proj], 0)
    for level in range(live_count.bit_length() - 1):
        other_block = from_partner(mlp_blocks, "ctx", level)
        mlp_blocks = jnp.concatenate([mlp_blocks, other_block], axis=2)
    slots_per = max(2, 5 * tok_rows // (4 * live_count))
    chosen = expert_ids[:, 0]
    onehot = (chosen[:, None] == jnp.arange(live_count, dtype=jnp.int32)[None, :]).astype(
        jnp.bfloat16
    )
    row_iota = jnp.arange(tok_rows, dtype=jnp.int32)
    strictly_lower = (row_iota[None, :] < row_iota[:, None]).astype(jnp.bfloat16)
    counts_before = jnp.dot(strictly_lower, onehot, preferred_element_type=jnp.float32)
    slot_index = jnp.sum(onehot.astype(jnp.float32) * counts_before, axis=1).astype(jnp.int32)
    target_slot = chosen * slots_per + slot_index
    dispatch_matrix = (
        jnp.arange(live_count * slots_per, dtype=jnp.int32)[:, None] == target_slot[None, :]
    ).astype(jnp.bfloat16)
    packed = jnp.dot(dispatch_matrix, normed, preferred_element_type=jnp.float32).astype(
        jnp.bfloat16
    )
    sending = jnp.broadcast_to(
        packed.reshape(1, live_count, slots_per, width), (SPLIT, live_count, slots_per, width)
    )
    sending = sending.reshape(ctx_count, 1, slots_per, width)
    own_expert = device_index % live_count
    router_column = lax.dynamic_slice_in_dim(router, own_expert, 1, 1)
    weight_in = expert_in[0]
    weight_out = expert_out[0]
    received = lax.all_to_all(sending, "ctx", split_axis=0, concat_axis=1, tiled=True)
    rows = received.reshape(-1, width)
    expert_hidden = jax.nn.gelu(
        jnp.dot(rows, weight_in, preferred_element_type=jnp.float32)
    ).astype(jnp.bfloat16)
    mlp_hidden = jax.nn.gelu(
        jnp.dot(rows, mlp_blocks[0], preferred_element_type=jnp.float32)
    ).astype(jnp.bfloat16)
    gate = jax.nn.sigmoid(jnp.dot(rows, router_column, preferred_element_type=jnp.float32))
    produced = gate * jnp.dot(expert_hidden, weight_out, preferred_element_type=jnp.float32)
    produced = produced + lax.dot_general(
        mlp_hidden, mlp_blocks[1], (((1,), (1,)), ((), ())), preferred_element_type=jnp.float32
    )
    came_back = lax.all_to_all(
        produced.astype(jnp.bfloat16).reshape(received.shape),
        "ctx",
        split_axis=1,
        concat_axis=0,
        tiled=True,
    )
    summed = jnp.sum(
        came_back.astype(jnp.float32).reshape(SPLIT, live_count * slots_per, width), axis=0
    )
    mixture_part = lax.dot_general(
        dispatch_matrix.astype(jnp.float32),
        summed,
        (((0,), (0,)), ((), ())),
        precision=lax.Precision.HIGHEST,
        preferred_element_type=jnp.float32,
    )
    return (mixed + mixture_part).astype(jnp.bfloat16)


def swap(array, mask):
    return lax.ppermute(array, "ctx", [(i, i ^ mask) for i in range(lax.axis_size("ctx"))])


VMEM = pl.BlockSpec(memory_space=pltpu.VMEM)
SMEM = pl.BlockSpec(memory_space=pltpu.SMEM)


HBM = pl.BlockSpec(memory_space=pltpu.HBM)


def call(kernel, outs, specs, flops, mib, *operands, copies=0, scratch=()):
    return pl.pallas_call(
        kernel,
        out_shape=outs,
        in_specs=specs,
        out_specs=[VMEM] * len(outs),
        scratch_shapes=[*scratch] + ([pltpu.SemaphoreType.DMA((copies,))] if copies else []),
        compiler_params=pltpu.CompilerParams(vmem_limit_bytes=mib * 2**20),
        cost_estimate=pl.CostEstimate(
            flops=flops,
            bytes_accessed=sum(x.size * x.dtype.itemsize for x in operands),
            transcendentals=0,
        ),
    )(*operands)


def copy_all(pairs, sems):
    copies = [pltpu.make_async_copy(a, b, sems.at[at]) for at, (a, b) in enumerate(pairs)]
    for copy in copies:
        copy.start()
    for copy in copies:
        copy.wait()


def load_kernel(*refs):
    count = len(refs) // 2
    copy_all(zip(refs[:count], refs[count : 2 * count]), refs[-1])


def load(mib, *arrays):
    outs = [pltpu.VMEM(array.shape, array.dtype) for array in arrays]
    count = len(arrays)
    return call(load_kernel, outs, [HBM] * count, 0, mib, *arrays, copies=count)


def pack_kernel(index_ref, query_ref, key_ref, value_ref, *refs):
    pairs = []
    for at, out_ref in enumerate(refs[:-1]):
        head = (index_ref[0] ^ 2 * at) >> 1
        columns = pl.ds(pl.multiple_of(head * DH, DH), DH)
        for part, ref in enumerate((query_ref, key_ref, value_ref)):
            pairs.append((ref.at[:, columns], out_ref.at[:, pl.ds(part * DH, DH)]))
    copy_all(pairs, refs[-1])


def arrange_kernel(index_ref, *refs):
    query_ref, pair_ref = refs[-2:]
    for at, ref in enumerate(refs[:-2]):
        place = (index_ref[0] ^ 2 * at) >> 1
        query_ref[place] = ref[:, :DH]
        pair_ref[place] = ref[:, DH:]


def attention_kernel(index_ref, query_ref, own_ref, other_ref, ids_ref, *refs):
    out_refs, (held, ids, sem) = refs[:-3], refs[-3:]
    ids_copy = pltpu.make_async_copy(ids_ref, ids, sem.at[0])
    ids_copy.start()
    blocks, rows, _ = own_ref.shape
    row_at = lax.broadcasted_iota(jnp.int32, (rows, rows), 0)
    column_at = lax.broadcasted_iota(jnp.int32, (rows, rows), 1)
    causal = column_at <= row_at
    also = jnp.broadcast_to(index_ref[0] & 1 == 1, (rows, rows))
    contract = (((1,), (1,)), ((), ()))
    for block in range(blocks):
        query = query_ref[block]
        scores = []
        for ref, last_visible in ((own_ref, causal), (other_ref, also)):
            for at in range(block + 1):
                score = lax.dot_general(
                    query, ref[at, :, :DH], contract, preferred_element_type=jnp.float32
                ) * DH ** (-0.5)
                if at == block:
                    score = jnp.where(last_visible, score, NEG_FILL)
                scores.append(score)
        peak = scores[0]
        for score in scores[1:]:
            peak = jnp.maximum(peak, score)
        row_max = jnp.max(peak, axis=1, keepdims=True)
        numer = jnp.zeros((rows, DH), jnp.float32)
        summed = jnp.zeros((rows, rows), jnp.float32)
        for at, score in enumerate(scores):
            weights = jnp.exp(score - row_max)
            summed = summed + weights
            ref = own_ref if at <= block else other_ref
            numer = numer + jnp.dot(
                weights.astype(jnp.bfloat16),
                ref[at % (block + 1), :, DH:],
                preferred_element_type=jnp.float32,
            )
        totals = jnp.sum(summed, axis=1, keepdims=True)
        held[block] = (numer / totals).astype(jnp.bfloat16)
    ids_copy.wait()
    id_rows = jnp.broadcast_to(
        ids[...].astype(jnp.float32), (out_refs[0].shape[0] - rows, rows)
    ).astype(jnp.bfloat16)
    for at, out_ref in enumerate(out_refs):
        out_ref[:rows, :] = held[(index_ref[0] ^ 2 * at) >> 1]
        out_ref[rows:, :] = id_rows


def project_kernel(index_ref, weight_ref, resid_ref, gain_ref, *refs):
    heads_in, (mixed_ref, normed_ref, top_ref, bottom_ref, held) = refs[:-5], refs[-5:]
    rows = resid_ref.shape[0]
    for at, ref in enumerate(heads_in):
        held[(index_ref[0] ^ 2 * at) >> 1] = ref[:rows, :]
    attn = jnp.concatenate([held[head] for head in range(len(heads_in))], axis=1)
    mixed = resid_ref[...].astype(jnp.float32) + jnp.dot(
        attn, weight_ref[...], preferred_element_type=jnp.float32
    )
    mixed_ref[...] = mixed
    scale = lax.rsqrt(jnp.mean(mixed * mixed, axis=1, keepdims=True) + EPSILON)
    normed = (mixed * scale * gain_ref[...]).astype(jnp.bfloat16)
    normed_ref[...] = normed
    top_ref[...] = normed[: rows // 2]
    bottom_ref[...] = normed[rows // 2 :]


def mixture_kernel(
    start, index_ref, router_ref, up_a, up_b, in_a, in_b, down_a, down_b, out_a, out_b, *refs
):
    count = len(refs) // 3
    shards, ids_refs, out_refs = refs[:count], refs[count : 2 * count], refs[2 * count :]
    rows, width = shards[0].shape
    own = (index_ref[0] & 1).astype(jnp.float32)

    def expert(ref):
        count = ref.shape[1]
        ids = ref[count : count + 16, :].astype(jnp.float32)[0:1, :]
        column = jnp.transpose(jnp.broadcast_to(ids, (count, count)))[:, 0:1]
        return column[start : start + rows]

    normed = jnp.concatenate([ref[...] for ref in shards], axis=0)
    chosen = jnp.concatenate([expert(ref) for ref in ids_refs], axis=0)
    mine = chosen == own
    router = router_ref[...].astype(jnp.float32)
    column = jnp.where(chosen > 0, router[1:2, :], router[0:1, :])
    logits = jnp.sum(normed.astype(jnp.float32) * column, axis=1, keepdims=True)
    gate = jax.nn.sigmoid(logits)

    def hidden(weights):
        return jax.nn.gelu(jnp.dot(normed, weights[...], preferred_element_type=jnp.float32))

    mlp_a = hidden(up_a).astype(jnp.bfloat16)
    mlp_b = hidden(up_b).astype(jnp.bfloat16)
    exp_a = jnp.where(mine, hidden(in_a), 0.0).astype(jnp.bfloat16)
    exp_b = jnp.where(mine, 0.0, hidden(in_b)).astype(jnp.bfloat16)
    contract = (((1,), (1,)), ((), ()))
    step = min(width, 512)
    for begin in range(0, width, step):
        span = slice(begin, begin + step)
        part = gate * (
            jnp.dot(exp_a, out_a[:, span], preferred_element_type=jnp.float32)
            + jnp.dot(exp_b, out_b[:, span], preferred_element_type=jnp.float32)
        )
        part = part + (
            lax.dot_general(mlp_a, down_a[span, :], contract, preferred_element_type=jnp.float32)
            + lax.dot_general(mlp_b, down_b[span, :], contract, preferred_element_type=jnp.float32)
        )
        part = part.astype(jnp.bfloat16)
        for at, out_ref in enumerate(out_refs):
            out_ref[:, span] = part[at * rows : (at + 1) * rows]


def finish_kernel(mixed_ref, *refs):
    whole, split, out_ref = refs[:3], refs[3:-1], refs[-1]
    rows = mixed_ref.shape[0]
    for at in range(2):
        span = slice(at * rows // 2, (at + 1) * rows // 2)
        total = mixed_ref[span, :]
        for ref in whole:
            total = total + ref[span, :].astype(jnp.float32)
        for ref in split[at::2]:
            total = total + ref[...].astype(jnp.float32)
        out_ref[span, :] = total.astype(jnp.bfloat16)


def body_by_pairs(
    queries,
    keys,
    values,
    resid,
    out_proj,
    norm_gain,
    up_proj,
    down_proj,
    router,
    expert_ids,
    expert_in,
    expert_out,
):
    rows, width = resid.shape
    heads = queries.shape[1] // DH
    ctx_count = lax.axis_size("ctx")
    device_index = lax.axis_index("ctx")
    index = device_index.reshape(1)
    shape = jax.ShapeDtypeStruct
    packed = call(
        pack_kernel,
        [pltpu.VMEM((rows, 3 * DH), jnp.bfloat16)] * heads,
        [SMEM] + [HBM] * 3,
        0,
        62,
        index,
        queries,
        keys,
        values,
        copies=3 * heads,
    )
    blocks = [packed[0]] + [swap(packed[at], 2 * at) for at in range(1, heads)]
    query, own = call(
        arrange_kernel,
        [shape((heads, rows, DH), jnp.bfloat16), shape((heads, rows, 2 * DH), jnp.bfloat16)],
        [SMEM] + [VMEM] * heads,
        0,
        8,
        index,
        *blocks,
    )
    other = swap(own, 1)
    weights_own = (up_proj, expert_in[0], down_proj, expert_out[0])
    weights_other = [swap(array, 1) for array in weights_own]
    *weights_own, out_weight, resid_rows = load(44, *weights_own, out_proj, resid)
    weights = tuple(w for pair in zip(weights_own, weights_other) for w in pair)
    outs = call(
        attention_kernel,
        [pltpu.VMEM((rows + 16, DH), jnp.bfloat16)] * heads,
        [SMEM] + [VMEM] * 3 + [HBM],
        10**9,
        12,
        index,
        query,
        own,
        other,
        expert_ids.reshape(1, rows),
        copies=1,
        scratch=[pltpu.VMEM((heads, rows, DH), jnp.bfloat16), pltpu.VMEM((1, rows), jnp.int32)],
    )
    backs = [outs[0]] + [swap(outs[at], 2 * at) for at in range(1, heads)]
    mixed, normed, *halves = call(
        project_kernel,
        [pltpu.VMEM((rows, width), jnp.float32), pltpu.VMEM((rows, width), jnp.bfloat16)]
        + [pltpu.VMEM((rows // 2, width), jnp.bfloat16)] * 2,
        [SMEM] + [VMEM] * (heads + 3),
        2 * out_proj.size * rows,
        12,
        index,
        out_weight,
        resid_rows,
        norm_gain.reshape(1, width),
        *backs,
        scratch=[pltpu.VMEM((heads, rows, DH), jnp.bfloat16)],
    )
    units = sum(w.size for w in weights[:4]) // width

    def mix(shards, start=0):
        count = next(iter(shards.values())).shape[0]
        return call(
            functools.partial(mixture_kernel, start),
            [pltpu.VMEM((count, width), jnp.bfloat16)] * len(shards),
            [SMEM] + [VMEM] * (9 + 2 * len(shards)),
            4 * len(shards) * count * width * units,
            16,
            index,
            router.T,
            *weights,
            *shards.values(),
            *(backs[offset // 2] for offset in shards),
        )

    def plus(first, second):
        return (first.astype(jnp.float32) + second.astype(jnp.float32)).astype(jnp.bfloat16)

    far = [4 * at for at in range(ctx_count // 4 - 1, 1, -1)]
    across = swap(normed, 2)
    beside = swap(normed, 4)
    beside_across = swap(across, 4)
    arrived = []
    for offset in far:
        for half, rows_sent in zip("ab", halves):
            first = swap(rows_sent, offset)
            second = swap(first, 2)
            start = 0 if half == "a" else rows // 2
            part, part_across = mix({offset: first, offset | 2: second}, start)
            summed = plus(part, swap(part_across, 2))
            arrived.append(swap(summed, offset))
    part, part_across = mix({0: normed, 2: across})
    part_beside, part_both = mix({4: beside, 6: beside_across})
    summed = plus(part_across, swap(part_both, 4))
    (result,) = call(
        finish_kernel,
        [shape((rows, width), jnp.bfloat16)],
        [VMEM] * (4 + len(arrived)),
        0,
        12,
        mixed,
        part,
        swap(part_beside, 4),
        swap(summed, 2),
        *arrived,
    )
    return result


def solution(mesh):
    ctx_count = mesh.shape["ctx"]

    def by_pairs(args):
        queries, router = args[0], args[8]
        return (
            router.shape[1] == 2
            and ctx_count == 2 * SPLIT
            and queries.shape[1] == ctx_count // 2 * DH
            and ctx_count % 4 == 0
            and ctx_count & (ctx_count - 1) == 0
        )

    def chosen(*args):
        if not by_pairs(args):
            return body(*args)
        return body_by_pairs(*args)

    placed = (
        P(("groups", "ctx"), None),
        P(("groups", "ctx"), None),
        P(("groups", "ctx"), None),
        P(("groups", "ctx"), None),
        P(),
        P(),
        P(None, "ctx"),
        P(None, "ctx"),
        P(),
        P(("groups", "ctx"), None),
        P("ctx", None, None),
        P("ctx", None, None),
    )
    return jax.shard_map(
        chosen, mesh=mesh, in_specs=placed, out_specs=P(("groups", "ctx"), None), check_vma=False
    )
```

profile of v0, /device:TPU:1, one launch (start us, length us, event | category | flops | bytes accessed | tf_op | source)
XLA Modules:
  0.0 186.3 jit_solution(4302623147061283)
XLA Ops:
  1.3 2.1 %collective-permute-start = (bf16[128,384]{1,0:T(8,128)(2,1)S(1)}, bf16[128,384]{1,0:T(8,128)(2,1)S(1)}, u32[]{:S(2)}, u32[]{:S(2)}) collective-permute-start(bf16[128,384]{1,0:T(8,128)(2,1)S(1)} %get-tuple-element.48), channel_id=1, source_target_pairs={{0,2},{1,3},{2,0},{3,1},{4,6},{5,7},{6,4},{7,5},{8,10},{9,11},{10,... | collective-permute-start | bytes 294920 | tf_op jit(solution)/shard_map/ppermute | solution.py:180
  4.7 2.4 %collective-permute-start.3 = (bf16[128,384]{1,0:T(8,128)(2,1)S(1)}, bf16[128,384]{1,0:T(8,128)(2,1)S(1)}, u32[]{:S(2)}, u32[]{:S(2)}) collective-permute-start(bf16[128,384]{1,0:T(8,128)(2,1)S(1)} %get-tuple-element.51), channel_id=1, source_target_pairs={{0,8},{1,9},{2,10},{3,11},{4,12},{5,13},{6,14},{7,15},{8,0},{9,1},... | collective-permute-start | bytes 294920 | tf_op jit(solution)/shard_map/ppermute | solution.py:180
  8.2 3.3 %collective-permute-start.5 = (bf16[128,384]{1,0:T(8,128)(2,1)S(1)}, bf16[128,384]{1,0:T(8,128)(2,1)S(1)}, u32[]{:S(2)}, u32[]{:S(2)}) collective-permute-start(bf16[128,384]{1,0:T(8,128)(2,1)S(1)} %get-tuple-element.53), channel_id=1, source_target_pairs={{0,12},{1,13},{2,14},{3,15},{4,8},{5,9},{6,10},{7,11},{8,4},{9,5},... | collective-permute-start | bytes 294920 | tf_op jit(solution)/shard_map/ppermute | solution.py:180
  11.5 10.7 %collective-permute-done.4.refs_5_ = bf16[128,384]{1,0:T(8,128)(2,1)S(1)} collective-permute-done((bf16[128,384]{1,0:T(8,128)(2,1)S(1)}, bf16[128,384]{1,0:T(8,128)(2,1)S(1)}, u32[]{:S(2)}, u32[]{:S(2)}) %collective-permute-start.4) | collective-permute-done | bytes 98336 | tf_op jit(solution)/shard_map/ppermute | solution.py:180
  22.3 2.0 %collective-permute-start.7 = (bf16[8,128,256]{2,1,0:T(8,128)(2,1)S(1)}, bf16[8,128,256]{2,1,0:T(8,128)(2,1)S(1)}, u32[]{:S(2)}, u32[]{:S(2)}) collective-permute-start(bf16[8,128,256]{2,1,0:T(8,128)(2,1)S(1)} %get-tuple-element.56.own_ref), channel_id=1, source_target_pairs={{0,1},{1,0},{2,3},{3,2},{4,5},{5,4},{6,7},{7,6},{8,9},{9,8},{10,11... | collective-permute-start | bytes 1572872 | tf_op jit(solution)/shard_map/ppermute | solution.py:180
  26.5 4.2 %shard_map.121 = (bf16[144,128]{1,0:T(8,128)(2,1)S(1)}, bf16[144,128]{1,0:T(8,128)(2,1)S(1)}, bf16[144,128]{1,0:T(8,128)(2,1)S(1)}, bf16[144,128]{1,0:T(8,128)(2...) custom-call(s32[1]{0:T(128)} %bitcast.index_ref, ...), custom_call_target="tpu_custom_call" | custom-call | flops 1000000000 | bytes 1311236 | tf_op jit(solution)/shard_map/pallas_call | solution.py:191
  31.4 3.4 %collective-permute-start.9 = (bf16[144,128]{1,0:T(8,128)(2,1)S(1)}, bf16[144,128]{1,0:T(8,128)(2,1)S(1)}, u32[]{:S(2)}, u32[]{:S(2)}) collective-permute-start(bf16[144,128]{1,0:T(8,128)(2,1)S(1)} %get-tuple-element.59), channel_id=1, source_target_pairs={{0,4},{1,5},{2,6},{3,7},{4,0},{5,1},{6,2},{7,3},{8,12},{9,13},{10,... | collective-permute-start | bytes 110600 | tf_op jit(solution)/shard_map/ppermute | solution.py:180
  35.6 2.8 %collective-permute-start.11 = (bf16[144,128]{1,0:T(8,128)(2,1)S(1)}, bf16[144,128]{1,0:T(8,128)(2,1)S(1)}, u32[]{:S(2)}, u32[]{:S(2)}) collective-permute-start(bf16[144,128]{1,0:T(8,128)(2,1)S(1)} %get-tuple-element.61), channel_id=1, source_target_pairs={{0,8},{1,9},{2,10},{3,11},{4,12},{5,13},{6,14},{7,15},{8,0},{9,1},... | collective-permute-start | bytes 110600 | tf_op jit(solution)/shard_map/ppermute | solution.py:180
  40.8 2.1 %collective-permute-start.14 = (bf16[144,128]{1,0:T(8,128)(2,1)S(1)}, bf16[144,128]{1,0:T(8,128)(2,1)S(1)}, u32[]{:S(2)}, u32[]{:S(2)}) collective-permute-start(bf16[144,128]{1,0:T(8,128)(2,1)S(1)} %get-tuple-element.64), channel_id=1, source_target_pairs={{0,14},{1,15},{2,12},{3,13},{4,10},{5,11},{6,8},{7,9},{8,6},{9,7},... | collective-permute-start | bytes 110600 | tf_op jit(solution)/shard_map/ppermute | solution.py:180
  42.9 4.2 %shard_map.118 = (bf16[2048,256]{1,0:T(8,128)(2,1)S(1)}, bf16[2048,512]{1,0:T(8,128)(2,1)S(1)}, bf16[2048,256]{1,0:T(8,128)(2,1)S(1)}, bf16[512,2048]{1,0:T(8,12...) custom-call(bf16[2048,256]{1,0:T(8,128)(2,1)} %refs_0_.1, bf16[2048,512]{1,0:T(8,128)(2,1)} %bitcast.15, ...), custom_call_target="tpu_custom_call" | custom-call | bytes 11010048 | tf_op jit(solution)/shard_map/pallas_call | solution.py:191
  48.0 2.1 %collective-permute-start.25 = (bf16[64,2048]{1,0:T(8,128)(2,1)S(1)}, bf16[64,2048]{1,0:T(8,128)(2,1)S(1)}, u32[]{:S(2)}, u32[]{:S(2)}) collective-permute-start(bf16[64,2048]{1,0:T(8,128)(2,1)S(1)} %get-tuple-element.75), channel_id=1, source_target_pairs={{0,12},{1,13},{2,14},{3,15},{4,8},{5,9},{6,10},{7,11},{8,4},{9,5},... | collective-permute-start | bytes 786440 | tf_op jit(solution)/shard_map/ppermute | solution.py:180
  51.4 3.4 %collective-permute-start.15 = (bf16[2048,256]{1,0:T(8,128)(2,1)S(1)}, bf16[2048,256]{1,0:T(8,128)(2,1)S(1)}, u32[]{:S(2)}, u32[]{:S(2)}) collective-permute-start(bf16[2048,256]{1,0:T(8,128)(2,1)S(1)} %copy-done.3), channel_id=1, source_target_pairs={{0,1},{1,0},{2,3},{3,2},{4,5},{5,4},{6,7},{7,6},{8,9},{9,8},{10,11... | collective-permute-start | bytes 3145736 | tf_op jit(solution)/shard_map/ppermute | solution.py:180
  55.2 9.9 %collective-permute-start.33 = (bf16[64,2048]{1,0:T(8,128)(2,1)S(1)}, bf16[64,2048]{1,0:T(8,128)(2,1)S(1)}, u32[]{:S(2)}, u32[]{:S(2)}) collective-permute-start(bf16[64,2048]{1,0:T(8,128)(2,1)S(1)} %get-tuple-element.75), channel_id=1, source_target_pairs={{0,8},{1,9},{2,10},{3,11},{4,12},{5,13},{6,14},{7,15},{8,0},{9,1},... | collective-permute-start | bytes 786440 | tf_op jit(solution)/shard_map/ppermute | solution.py:180
  65.2 8.4 %collective-permute-start.37 = (bf16[64,2048]{1,0:T(8,128)(2,1)S(1)}, bf16[64,2048]{1,0:T(8,128)(2,1)S(1)}, u32[]{:S(2)}, u32[]{:S(2)}) collective-permute-start(bf16[64,2048]{1,0:T(8,128)(2,1)S(1)} %get-tuple-element.78), channel_id=1, source_target_pairs={{0,8},{1,9},{2,10},{3,11},{4,12},{5,13},{6,14},{7,15},{8,0},{9,1},... | collective-permute-start | bytes 786440 | tf_op jit(solution)/shard_map/ppermute | solution.py:180
  73.6 10.5 %collective-permute-done.33.refs_0_ = bf16[64,2048]{1,0:T(8,128)(2,1)S(1)} collective-permute-done((bf16[64,2048]{1,0:T(8,128)(2,1)S(1)}, bf16[64,2048]{1,0:T(8,128)(2,1)S(1)}, u32[]{:S(2)}, u32[]{:S(2)}) %collective-permute-start.33) | collective-permute-done | bytes 262176 | tf_op jit(solution)/shard_map/ppermute | solution.py:180
  84.0 8.4 %collective-permute-start.17 = (bf16[2048,256]{1,0:T(8,128)(2,1)S(1)}, bf16[2048,256]{1,0:T(8,128)(2,1)S(1)}, u32[]{:S(2)}, u32[]{:S(2)}) collective-permute-start(bf16[2048,256]{1,0:T(8,128)(2,1)S(1)} %copy-done.4), channel_id=1, source_target_pairs={{0,1},{1,0},{2,3},{3,2},{4,5},{5,4},{6,7},{7,6},{8,9},{9,8},{10,11... | collective-permute-start | bytes 3145736 | tf_op jit(solution)/shard_map/ppermute | solution.py:180
  93.7 9.3 %collective-permute-done.19.refs_1_ = bf16[128,2048]{1,0:T(8,128)(2,1)S(1)} collective-permute-done((bf16[128,2048]{1,0:T(8,128)(2,1)S(1)}, bf16[128,2048]{1,0:T(8,128)(2,1)S(1)}, u32[]{:S(2)}, u32[]{:S(2)}) %collective-permute-start.19) | collective-permute-done | bytes 524320 | tf_op jit(solution)/shard_map/ppermute | solution.py:180
  104.4 11.3 %collective-permute-done.21.refs_1_ = bf16[128,2048]{1,0:T(8,128)(2,1)S(1)} collective-permute-done((bf16[128,2048]{1,0:T(8,128)(2,1)S(1)}, bf16[128,2048]{1,0:T(8,128)(2,1)S(1)}, u32[]{:S(2)}, u32[]{:S(2)}) %collective-permute-start.21) | collective-permute-done | bytes 524320 | tf_op jit(solution)/shard_map/ppermute | solution.py:180
  115.7 1.5 collective-permute-start.38
  117.2 3.9 %shard_map.124 = (bf16[128,2048]{1,0:T(8,128)(2,1)S(1)}, bf16[128,2048]{1,0:T(8,128)(2,1)S(1)}) custom-call(s32[1]{0:T(128)} %bitcast.index_ref, bf16[2,2048]{1,0:T(2,128)(2,1)S(1)} %bitcast.6, bf16[2048,256]{1,0:T(8,128)(2,1)S(1)} %get-tuple-element.66.up_a, bf16[2048,256]{1,0:T(8,128)(2,1)S(1)} %collective-permute-done.15.up_b, ...), custom_call_target="tpu_custom_call" | custom-call | flops 3221225472 | bytes 13713412 | tf_op jit(solution)/shard_map/pallas_call | solution.py:191
  122.7 2.6 %shard_map.125 = (bf16[64,2048]{1,0:T(8,128)(2,1)S(1)}, bf16[64,2048]{1,0:T(8,128)(2,1)S(1)}) custom-call(s32[1]{0:T(128)} %bitcast.index_ref, bf16[2,2048]{1,0:T(2,128)(2,1)S(1)} %bitcast.7, bf16[2048,256]{1,0:T(8,128)(2,1)S(1)} %get-tuple-element.66.up_a, bf16[2048,256]{1,0:T(8,128)(2,1)S(1)} %collective-permute-done.15.up_b, ...), custom_call_target="tpu_custom_call" | custom-call | flops 1610612736 | bytes 13189124 | tf_op jit(solution)/shard_map/pallas_call | solution.py:191
  125.4 2.8 %shard_map.126 = (bf16[64,2048]{1,0:T(8,128)(2,1)S(1)}, bf16[64,2048]{1,0:T(8,128)(2,1)S(1)}) custom-call(s32[1]{0:T(128)} %bitcast.index_ref, bf16[2,2048]{1,0:T(2,128)(2,1)S(1)} %bitcast.8, bf16[2048,256]{1,0:T(8,128)(2,1)S(1)} %get-tuple-element.66.up_a, bf16[2048,256]{1,0:T(8,128)(2,1)S(1)} %collective-permute-done.15.up_b, ...), custom_call_target="tpu_custom_call" | custom-call | flops 1610612736 | bytes 13189124 | tf_op jit(solution)/shard_map/pallas_call | solution.py:191
  128.2 1.5 collective-permute-start.31
  129.7 2.6 %shard_map.127 = (bf16[64,2048]{1,0:T(8,128)(2,1)S(1)}, bf16[64,2048]{1,0:T(8,128)(2,1)S(1)}) custom-call(s32[1]{0:T(128)} %bitcast.index_ref, bf16[2,2048]{1,0:T(2,128)(2,1)S(1)} %bitcast.9, bf16[2048,256]{1,0:T(8,128)(2,1)S(1)} %get-tuple-element.66.up_a, bf16[2048,256]{1,0:T(8,128)(2,1)S(1)} %collective-permute-done.15.up_b, ...), custom_call_target="tpu_custom_call" | custom-call | flops 1610612736 | bytes 13189124 | tf_op jit(solution)/shard_map/pallas_call | solution.py:191
  132.4 2.6 %shard_map.128 = (bf16[64,2048]{1,0:T(8,128)(2,1)S(1)}, bf16[64,2048]{1,0:T(8,128)(2,1)S(1)}) custom-call(s32[1]{0:T(128)} %bitcast.index_ref, bf16[2,2048]{1,0:T(2,128)(2,1)S(1)} %bitcast.10, bf16[2048,256]{1,0:T(8,128)(2,1)S(1)} %get-tuple-element.66.up_a, bf16[2048,256]{1,0:T(8,128)(2,1)S(1)} %collective-permute-done.15.up_b, ...), custom_call_target="tpu_custom_call" | custom-call | flops 1610612736 | bytes 13189124 | tf_op jit(solution)/shard_map/pallas_call | solution.py:191
  135.0 3.9 %shard_map.123 = (bf16[128,2048]{1,0:T(8,128)(2,1)S(1)}, bf16[128,2048]{1,0:T(8,128)(2,1)S(1)}) custom-call(s32[1]{0:T(128)} %bitcast.index_ref, bf16[2,2048]{1,0:T(2,128)(2,1)S(1)} %bitcast.11, bf16[2048,256]{1,0:T(8,128)(2,1)S(1)} %get-tuple-element.66.up_a, bf16[2048,256]{1,0:T(8,128)(2,1)S(1)} %collective-permute-done.15.up_b, ...), custom_call_target="tpu_custom_call" | custom-call | flops 3221225472 | bytes 13713412 | tf_op jit(solution)/shard_map/pallas_call | solution.py:191
  138.9 1.5 collective-permute-start.39
  145.3 3.3 %collective-permute-done.39 = bf16[64,2048]{1,0:T(8,128)(2,1)S(1)} collective-permute-done((bf16[64,2048]{1,0:T(8,128)(2,1)S(1)}, bf16[64,2048]{1,0:T(8,128)(2,1)S(1)}, u32[]{:S(2)}, u32[]{:S(2)}) %collective-permute-start.39) | collective-permute-done | bytes 262176 | tf_op jit(solution)/shard_map/ppermute | solution.py:180
  149.3 1.5 collective-permute-start.40
  150.8 1.7 collective-permute-done.32.refs_4_
  152.5 26.7 %collective-permute-done.36.refs_5_ = bf16[64,2048]{1,0:T(8,128)(2,1)S(1)} collective-permute-done((bf16[64,2048]{1,0:T(8,128)(2,1)S(1)}, bf16[64,2048]{1,0:T(8,128)(2,1)S(1)}, u32[]{:S(2)}, u32[]{:S(2)}) %collective-permute-start.36) | collective-permute-done | bytes 262176 | tf_op jit(solution)/shard_map/ppermute | solution.py:180
  179.2 5.9 %collective-permute-done.40.refs_6_ = bf16[64,2048]{1,0:T(8,128)(2,1)S(1)} collective-permute-done((bf16[64,2048]{1,0:T(8,128)(2,1)S(1)}, bf16[64,2048]{1,0:T(8,128)(2,1)S(1)}, u32[]{:S(2)}, u32[]{:S(2)}) %collective-permute-start.40) | collective-permute-done | bytes 262176 | tf_op jit(solution)/shard_map/ppermute | solution.py:180
  (77 shorter events, 23.6 us)
Async XLA Ops:
  3.4 8.1 %collective-permute-start.1 = (bf16[128,384]{1,0:T(8,128)(2,1)S(1)}, bf16[128,384]{1,0:T(8,128)(2,1)S(1)}, u32[]{:S(2)}, u32[]{:S(2)}) collective-permute-start(bf16[128,384]{1,0:T(8,128)(2,1)S(1)} %get-tuple-element.49), channel_id=1, source_target_pairs={{0,4},{1,5},{2,6},{3,7},{4,0},{5,1},{6,2},{7,3},{8,12},{9,13},{10,... | collective-permute-start | bytes 294920 | tf_op jit(solution)/shard_map/ppermute | solution.py:180
  7.2 15.0 %collective-permute-start.4 = (bf16[128,384]{1,0:T(8,128)(2,1)S(1)}, bf16[128,384]{1,0:T(8,128)(2,1)S(1)}, u32[]{:S(2)}, u32[]{:S(2)}) collective-permute-start(bf16[128,384]{1,0:T(8,128)(2,1)S(1)} %get-tuple-element.52), channel_id=1, source_target_pairs={{0,10},{1,11},{2,8},{3,9},{4,14},{5,15},{6,12},{7,13},{8,2},{9,3},... | collective-permute-start | bytes 294920 | tf_op jit(solution)/shard_map/ppermute | solution.py:180
  8.2 14.0 %collective-permute-start.5 = (bf16[128,384]{1,0:T(8,128)(2,1)S(1)}, bf16[128,384]{1,0:T(8,128)(2,1)S(1)}, u32[]{:S(2)}, u32[]{:S(2)}) collective-permute-start(bf16[128,384]{1,0:T(8,128)(2,1)S(1)} %get-tuple-element.53), channel_id=1, source_target_pairs={{0,12},{1,13},{2,14},{3,15},{4,8},{5,9},{6,10},{7,11},{8,4},{9,5},... | collective-permute-start | bytes 294920 | tf_op jit(solution)/shard_map/ppermute | solution.py:180
  11.5 10.7 %collective-permute-start.6 = (bf16[128,384]{1,0:T(8,128)(2,1)S(1)}, bf16[128,384]{1,0:T(8,128)(2,1)S(1)}, u32[]{:S(2)}, u32[]{:S(2)}) collective-permute-start(bf16[128,384]{1,0:T(8,128)(2,1)S(1)} %get-tuple-element.54), channel_id=1, source_target_pairs={{0,14},{1,15},{2,12},{3,13},{4,10},{5,11},{6,8},{7,9},{8,6},{9,7},... | collective-permute-start | bytes 294920 | tf_op jit(solution)/shard_map/ppermute | solution.py:180
  24.3 91.4 %collective-permute-start.16 = (bf16[2048,512]{1,0:T(8,128)(2,1)}, bf16[2048,512]{1,0:T(8,128)(2,1)S(1)}, u32[]{:S(2)}, u32[]{:S(2)}) collective-permute-start(bf16[2048,512]{1,0:T(8,128)(2,1)} %bitcast.14), channel_id=1, source_target_pairs={{0,1},{1,0},{2,3},{3,2},{4,5},{5,4},{6,7},{7,6},{8,9},{9,8},{10,11... | collective-permute-start | bytes 6291464 | tf_op jit(solution)/shard_map/ppermute | solution.py:180
  24.4 92.8 %collective-permute-start.18 = (bf16[512,2048]{1,0:T(8,128)(2,1)}, bf16[512,2048]{1,0:T(8,128)(2,1)S(1)}, u32[]{:S(2)}, u32[]{:S(2)}) collective-permute-start(bf16[512,2048]{1,0:T(8,128)(2,1)} %bitcast.16), channel_id=1, source_target_pairs={{0,1},{1,0},{2,3},{3,2},{4,5},{5,4},{6,7},{7,6},{8,9},{9,8},{10,11... | collective-permute-start | bytes 6291464 | tf_op jit(solution)/shard_map/ppermute | solution.py:180
  38.4 8.6 %collective-permute-start.12 = (bf16[144,128]{1,0:T(8,128)(2,1)S(1)}, bf16[144,128]{1,0:T(8,128)(2,1)S(1)}, u32[]{:S(2)}, u32[]{:S(2)}) collective-permute-start(bf16[144,128]{1,0:T(8,128)(2,1)S(1)} %get-tuple-element.62), channel_id=1, source_target_pairs={{0,10},{1,11},{2,8},{3,9},{4,14},{5,15},{6,12},{7,13},{8,2},{9,3},... | collective-permute-start | bytes 110600 | tf_op jit(solution)/shard_map/ppermute | solution.py:180
  39.6 7.5 %collective-permute-start.13 = (bf16[144,128]{1,0:T(8,128)(2,1)S(1)}, bf16[144,128]{1,0:T(8,128)(2,1)S(1)}, u32[]{:S(2)}, u32[]{:S(2)}) collective-permute-start(bf16[144,128]{1,0:T(8,128)(2,1)S(1)} %get-tuple-element.63), channel_id=1, source_target_pairs={{0,12},{1,13},{2,14},{3,15},{4,8},{5,9},{6,10},{7,11},{8,4},{9,5},... | collective-permute-start | bytes 110600 | tf_op jit(solution)/shard_map/ppermute | solution.py:180
  48.0 7.2 %collective-permute-start.25 = (bf16[64,2048]{1,0:T(8,128)(2,1)S(1)}, bf16[64,2048]{1,0:T(8,128)(2,1)S(1)}, u32[]{:S(2)}, u32[]{:S(2)}) collective-permute-start(bf16[64,2048]{1,0:T(8,128)(2,1)S(1)} %get-tuple-element.75), channel_id=1, source_target_pairs={{0,12},{1,13},{2,14},{3,15},{4,8},{5,9},{6,10},{7,11},{8,4},{9,5},... | collective-permute-start | bytes 786440 | tf_op jit(solution)/shard_map/ppermute | solution.py:180
  50.2 15.0 %collective-permute-start.29 = (bf16[64,2048]{1,0:T(8,128)(2,1)S(1)}, bf16[64,2048]{1,0:T(8,128)(2,1)S(1)}, u32[]{:S(2)}, u32[]{:S(2)}) collective-permute-start(bf16[64,2048]{1,0:T(8,128)(2,1)S(1)} %get-tuple-element.78), channel_id=1, source_target_pairs={{0,12},{1,13},{2,14},{3,15},{4,8},{5,9},{6,10},{7,11},{8,4},{9,5},... | collective-permute-start | bytes 786440 | tf_op jit(solution)/shard_map/ppermute | solution.py:180
  51.4 42.3 %collective-permute-start.15 = (bf16[2048,256]{1,0:T(8,128)(2,1)S(1)}, bf16[2048,256]{1,0:T(8,128)(2,1)S(1)}, u32[]{:S(2)}, u32[]{:S(2)}) collective-permute-start(bf16[2048,256]{1,0:T(8,128)(2,1)S(1)} %copy-done.3), channel_id=1, source_target_pairs={{0,1},{1,0},{2,3},{3,2},{4,5},{5,4},{6,7},{7,6},{8,9},{9,8},{10,11... | collective-permute-start | bytes 3145736 | tf_op jit(solution)/shard_map/ppermute | solution.py:180
  55.2 28.8 %collective-permute-start.33 = (bf16[64,2048]{1,0:T(8,128)(2,1)S(1)}, bf16[64,2048]{1,0:T(8,128)(2,1)S(1)}, u32[]{:S(2)}, u32[]{:S(2)}) collective-permute-start(bf16[64,2048]{1,0:T(8,128)(2,1)S(1)} %get-tuple-element.75), channel_id=1, source_target_pairs={{0,8},{1,9},{2,10},{3,11},{4,12},{5,13},{6,14},{7,15},{8,0},{9,1},... | collective-permute-start | bytes 786440 | tf_op jit(solution)/shard_map/ppermute | solution.py:180
  65.2 27.3 %collective-permute-start.37 = (bf16[64,2048]{1,0:T(8,128)(2,1)S(1)}, bf16[64,2048]{1,0:T(8,128)(2,1)S(1)}, u32[]{:S(2)}, u32[]{:S(2)}) collective-permute-start(bf16[64,2048]{1,0:T(8,128)(2,1)S(1)} %get-tuple-element.78), channel_id=1, source_target_pairs={{0,8},{1,9},{2,10},{3,11},{4,12},{5,13},{6,14},{7,15},{8,0},{9,1},... | collective-permute-start | bytes 786440 | tf_op jit(solution)/shard_map/ppermute | solution.py:180
  84.0 18.9 %collective-permute-start.17 = (bf16[2048,256]{1,0:T(8,128)(2,1)S(1)}, bf16[2048,256]{1,0:T(8,128)(2,1)S(1)}, u32[]{:S(2)}, u32[]{:S(2)}) collective-permute-start(bf16[2048,256]{1,0:T(8,128)(2,1)S(1)} %copy-done.4), channel_id=1, source_target_pairs={{0,1},{1,0},{2,3},{3,2},{4,5},{5,4},{6,7},{7,6},{8,9},{9,8},{10,11... | collective-permute-start | bytes 3145736 | tf_op jit(solution)/shard_map/ppermute | solution.py:180
  92.5 10.5 %collective-permute-start.19 = (bf16[128,2048]{1,0:T(8,128)(2,1)S(1)}, bf16[128,2048]{1,0:T(8,128)(2,1)S(1)}, u32[]{:S(2)}, u32[]{:S(2)}) collective-permute-start(bf16[128,2048]{1,0:T(8,128)(2,1)S(1)} %get-tuple-element.70.refs_0_), channel_id=1, source_target_pairs={{0,2},{1,3},{2,0},{3,1},{4,6},{5,7},{6,4},{7,5},{8,10},{9,11},{10,... | collective-permute-start | bytes 1572872 | tf_op jit(solution)/shard_map/ppermute | solution.py:180
  93.7 10.5 %collective-permute-start.20 = (bf16[128,2048]{1,0:T(8,128)(2,1)S(1)}, bf16[128,2048]{1,0:T(8,128)(2,1)S(1)}, u32[]{:S(2)}, u32[]{:S(2)}) collective-permute-start(bf16[128,2048]{1,0:T(8,128)(2,1)S(1)} %get-tuple-element.70.refs_0_), channel_id=1, source_target_pairs={{0,4},{1,5},{2,6},{3,7},{4,0},{5,1},{6,2},{7,3},{8,12},{9,13},{10,... | collective-permute-start | bytes 1572872 | tf_op jit(solution)/shard_map/ppermute | solution.py:180
  102.9 12.8 %collective-permute-start.21 = (bf16[128,2048]{1,0:T(8,128)(2,1)S(1)}, bf16[128,2048]{1,0:T(8,128)(2,1)S(1)}, u32[]{:S(2)}, u32[]{:S(2)}) collective-permute-start(bf16[128,2048]{1,0:T(8,128)(2,1)S(1)} %collective-permute-done.19.refs_1_), channel_id=1, source_target_pairs={{0,4},{1,5},{2,6},{3,7},{4,0},{5,1},{6,2},{7,3},{8,12},{9,13},{10,... | collective-permute-start | bytes 1572872 | tf_op jit(solution)/shard_map/ppermute | solution.py:180
  103.0 18.5 %collective-permute-start.26 = (bf16[64,2048]{1,0:T(8,128)(2,1)S(1)}, bf16[64,2048]{1,0:T(8,128)(2,1)S(1)}, u32[]{:S(2)}, u32[]{:S(2)}) collective-permute-start(bf16[64,2048]{1,0:T(8,128)(2,1)S(1)} %collective-permute-done.25.refs_0_), channel_id=1, source_target_pairs={{0,2},{1,3},{2,0},{3,1},{4,6},{5,7},{6,4},{7,5},{8,10},{9,11},{10,... | collective-permute-start | bytes 786440 | tf_op jit(solution)/shard_map/ppermute | solution.py:180
  104.2 21.1 %collective-permute-start.30 = (bf16[64,2048]{1,0:T(8,128)(2,1)S(1)}, bf16[64,2048]{1,0:T(8,128)(2,1)S(1)}, u32[]{:S(2)}, u32[]{:S(2)}) collective-permute-start(bf16[64,2048]{1,0:T(8,128)(2,1)S(1)} %collective-permute-done.29.refs_0_), channel_id=1, source_target_pairs={{0,2},{1,3},{2,0},{3,1},{4,6},{5,7},{6,4},{7,5},{8,10},{9,11},{10,... | collective-permute-start | bytes 786440 | tf_op jit(solution)/shard_map/ppermute | solution.py:180
  115.7 12.4 %collective-permute-start.34 = (bf16[64,2048]{1,0:T(8,128)(2,1)S(1)}, bf16[64,2048]{1,0:T(8,128)(2,1)S(1)}, u32[]{:S(2)}, u32[]{:S(2)}) collective-permute-start(bf16[64,2048]{1,0:T(8,128)(2,1)S(1)} %collective-permute-done.33.refs_0_), channel_id=1, source_target_pairs={{0,2},{1,3},{2,0},{3,1},{4,6},{5,7},{6,4},{7,5},{8,10},{9,11},{10,... | collective-permute-start | bytes 786440 | tf_op jit(solution)/shard_map/ppermute | solution.py:180
  115.7 16.5 %collective-permute-start.38 = (bf16[64,2048]{1,0:T(8,128)(2,1)S(1)}, bf16[64,2048]{1,0:T(8,128)(2,1)S(1)}, u32[]{:S(2)}, u32[]{:S(2)}) collective-permute-start(bf16[64,2048]{1,0:T(8,128)(2,1)S(1)} %collective-permute-done.37.refs_0_), channel_id=1, source_target_pairs={{0,2},{1,3},{2,0},{3,1},{4,6},{5,7},{6,4},{7,5},{8,10},{9,11},{10,... | collective-permute-start | bytes 786440 | tf_op jit(solution)/shard_map/ppermute | solution.py:180
  121.1 64.0 %collective-permute-start.22 = (bf16[128,2048]{1,0:T(8,128)(2,1)S(1)}, bf16[128,2048]{1,0:T(8,128)(2,1)S(1)}, u32[]{:S(2)}, u32[]{:S(2)}) collective-permute-start(bf16[128,2048]{1,0:T(8,128)(2,1)S(1)} %get-tuple-element.72), channel_id=1, source_target_pairs={{0,4},{1,5},{2,6},{3,7},{4,0},{5,1},{6,2},{7,3},{8,12},{9,13},{10,... | collective-permute-start | bytes 1572872 | tf_op jit(solution)/shard_map/ppermute | solution.py:180
  121.5 23.0 %collective-permute-start.23 = (bf16[128,2048]{1,0:T(8,128)(2,1)S(1)}, bf16[128,2048]{1,0:T(8,128)(2,1)S(1)}, u32[]{:S(2)}, u32[]{:S(2)}) collective-permute-start(bf16[128,2048]{1,0:T(8,128)(2,1)S(1)} %get-tuple-element.74), channel_id=1, source_target_pairs={{0,4},{1,5},{2,6},{3,7},{4,0},{5,1},{6,2},{7,3},{8,12},{9,13},{10,... | collective-permute-start | bytes 1572872 | tf_op jit(solution)/shard_map/ppermute | solution.py:180
  125.3 13.6 %collective-permute-start.27 = (bf16[64,2048]{1,0:T(8,128)(2,1)S(1)}, bf16[64,2048]{1,0:T(8,128)(2,1)S(1)}, u32[]{:S(2)}, u32[]{:S(2)}) collective-permute-start(bf16[64,2048]{1,0:T(8,128)(2,1)S(1)} %get-tuple-element.77), channel_id=1, source_target_pairs={{0,2},{1,3},{2,0},{3,1},{4,6},{5,7},{6,4},{7,5},{8,10},{9,11},{10,... | collective-permute-start | bytes 786440 | tf_op jit(solution)/shard_map/ppermute | solution.py:180
  128.2 12.3 %collective-permute-start.31 = (bf16[64,2048]{1,0:T(8,128)(2,1)S(1)}, bf16[64,2048]{1,0:T(8,128)(2,1)S(1)}, u32[]{:S(2)}, u32[]{:S(2)}) collective-permute-start(bf16[64,2048]{1,0:T(8,128)(2,1)S(1)} %get-tuple-element.80), channel_id=1, source_target_pairs={{0,2},{1,3},{2,0},{3,1},{4,6},{5,7},{6,4},{7,5},{8,10},{9,11},{10,... | collective-permute-start | bytes 786440 | tf_op jit(solution)/shard_map/ppermute | solution.py:180
  132.3 10.8 %collective-permute-start.35 = (bf16[64,2048]{1,0:T(8,128)(2,1)S(1)}, bf16[64,2048]{1,0:T(8,128)(2,1)S(1)}, u32[]{:S(2)}, u32[]{:S(2)}) collective-permute-start(bf16[64,2048]{1,0:T(8,128)(2,1)S(1)} %get-tuple-element.82), channel_id=1, source_target_pairs={{0,2},{1,3},{2,0},{3,1},{4,6},{5,7},{6,4},{7,5},{8,10},{9,11},{10,... | collective-permute-start | bytes 786440 | tf_op jit(solution)/shard_map/ppermute | solution.py:180
  138.9 9.8 %collective-permute-start.39 = (bf16[64,2048]{1,0:T(8,128)(2,1)S(1)}, bf16[64,2048]{1,0:T(8,128)(2,1)S(1)}, u32[]{:S(2)}, u32[]{:S(2)}) collective-permute-start(bf16[64,2048]{1,0:T(8,128)(2,1)S(1)} %get-tuple-element.84), channel_id=1, source_target_pairs={{0,2},{1,3},{2,0},{3,1},{4,6},{5,7},{6,4},{7,5},{8,10},{9,11},{10,... | collective-permute-start | bytes 786440 | tf_op jit(solution)/shard_map/ppermute | solution.py:180
  140.5 8.8 %collective-permute-start.28 = (bf16[64,2048]{1,0:T(8,128)(2,1)S(1)}, bf16[64,2048]{1,0:T(8,128)(2,1)S(1)}, u32[]{:S(2)}, u32[]{:S(2)}) collective-permute-start(bf16[64,2048]{1,0:T(8,128)(2,1)S(1)} %add_convert_fusion.4), channel_id=1, source_target_pairs={{0,12},{1,13},{2,14},{3,15},{4,8},{5,9},{6,10},{7,11},{8,4},{9,5},... | collective-permute-start | bytes 786440 | tf_op jit(solution)/shard_map/ppermute | solution.py:180
  143.0 9.5 %collective-permute-start.32 = (bf16[64,2048]{1,0:T(8,128)(2,1)S(1)}, bf16[64,2048]{1,0:T(8,128)(2,1)S(1)}, u32[]{:S(2)}, u32[]{:S(2)}) collective-permute-start(bf16[64,2048]{1,0:T(8,128)(2,1)S(1)} %add_convert_fusion.3), channel_id=1, source_target_pairs={{0,12},{1,13},{2,14},{3,15},{4,8},{5,9},{6,10},{7,11},{8,4},{9,5},... | collective-permute-start | bytes 786440 | tf_op jit(solution)/shard_map/ppermute | solution.py:180
  144.5 34.7 %collective-permute-start.36 = (bf16[64,2048]{1,0:T(8,128)(2,1)S(1)}, bf16[64,2048]{1,0:T(8,128)(2,1)S(1)}, u32[]{:S(2)}, u32[]{:S(2)}) collective-permute-start(bf16[64,2048]{1,0:T(8,128)(2,1)S(1)} %add_convert_fusion.2), channel_id=1, source_target_pairs={{0,8},{1,9},{2,10},{3,11},{4,12},{5,13},{6,14},{7,15},{8,0},{9,1},... | collective-permute-start | bytes 786440 | tf_op jit(solution)/shard_map/ppermute | solution.py:180
  148.7 36.5 %collective-permute-start.24 = (bf16[128,2048]{1,0:T(8,128)(2,1)S(1)}, bf16[128,2048]{1,0:T(8,128)(2,1)S(1)}, u32[]{:S(2)}, u32[]{:S(2)}) collective-permute-start(bf16[128,2048]{1,0:T(8,128)(2,1)S(1)} %add_convert_fusion), channel_id=1, source_target_pairs={{0,2},{1,3},{2,0},{3,1},{4,6},{5,7},{6,4},{7,5},{8,10},{9,11},{10,... | collective-permute-start | bytes 1572872 | tf_op jit(solution)/shard_map/ppermute | solution.py:180
  149.3 35.9 %collective-permute-start.40 = (bf16[64,2048]{1,0:T(8,128)(2,1)S(1)}, bf16[64,2048]{1,0:T(8,128)(2,1)S(1)}, u32[]{:S(2)}, u32[]{:S(2)}) collective-permute-start(bf16[64,2048]{1,0:T(8,128)(2,1)S(1)} %add_convert_fusion.1), channel_id=1, source_target_pairs={{0,8},{1,9},{2,10},{3,11},{4,12},{5,13},{6,14},{7,15},{8,0},{9,1},... | collective-permute-start | bytes 786440 | tf_op jit(solution)/shard_map/ppermute | solution.py:180
  (14 other events, 170.6 us)
where the time goes:
time: 190 us; the launch traced here: 186 us
  waiting for transfers between devices  82.4 us (43%)
  starting transfers between devices  72.4 us (38%)
  Pallas kernels  30.2 us (16%)
    ppermute x41, waiting for transfers between devices, swap(): lax.ppermute(array, 'ctx', [(i, i ^ mask) for i in range(lax.axis_size('c...  82.4 us
    ppermute x41, starting transfers between devices, swap(): lax.ppermute(array, 'ctx', [(i, i ^ mask) for i in range(lax.axis_size('c...  72.4 us
    pallas_call x12, Pallas kernels, call(): pl.pallas_call(kernel, out_shape=outs, in_specs=specs, out_specs=[VMEM] *...  30.2 us
  transfers between devices with their start and end apart: 41, of which 11 were waited for; matrix products, arithmetic and copies ran while one was open for 0% of the time, Pallas kernels for 15%

commit v1 on v0

--- a/solution.py
+++ b/solution.py
@@ -176,6 +176,9 @@
     return (mixed + mixture_part).astype(jnp.bfloat16)
 
 
+LOG2_E = 1.4426950408889634
+
+
 def swap(array, mask):
     return lax.ppermute(array, "ctx", [(i, i ^ mask) for i in range(lax.axis_size("ctx"))])
 
@@ -252,31 +255,28 @@
     contract = (((1,), (1,)), ((), ()))
     for block in range(blocks):
         query = query_ref[block]
-        scores = []
+        pair = []
         for ref, last_visible in ((own_ref, causal), (other_ref, also)):
-            for at in range(block + 1):
-                score = lax.dot_general(
-                    query, ref[at, :, :DH], contract, preferred_element_type=jnp.float32
-                ) * DH ** (-0.5)
-                if at == block:
-                    score = jnp.where(last_visible, score, NEG_FILL)
-                scores.append(score)
-        peak = scores[0]
-        for score in scores[1:]:
-            peak = jnp.maximum(peak, score)
-        row_max = jnp.max(peak, axis=1, keepdims=True)
-        numer = jnp.zeros((rows, DH), jnp.float32)
-        summed = jnp.zeros((rows, rows), jnp.float32)
-        for at, score in enumerate(scores):
-            weights = jnp.exp(score - row_max)
-            summed = summed + weights
-            ref = own_ref if at <= block else other_ref
+            seen = ref[: block + 1].reshape((block + 1) * rows, 2 * DH)
+            score = lax.dot_general(
+                query, seen[:, :DH], contract, preferred_element_type=jnp.float32
+            )
+            last = jnp.where(last_visible, score[:, block * rows :], NEG_FILL)
+            if block:
+                score = jnp.concatenate([score[:, : block * rows], last], axis=1)
+            else:
+                score = last
+            pair.append((score, seen[:, DH:]))
+        row_max = jnp.maximum(
+            *(jnp.max(score, axis=1, keepdims=True) for score, _ in pair)
+        )
+        numer, totals = 0.0, 0.0
+        for score, value in pair:
+            weights = jnp.exp2((score - row_max) * (DH ** (-0.5) * LOG2_E))
+            totals = totals + jnp.sum(weights, axis=1, keepdims=True)
             numer = numer + jnp.dot(
-                weights.astype(jnp.bfloat16),
-                ref[at % (block + 1), :, DH:],
-                preferred_element_type=jnp.float32,
+                weights.astype(jnp.bfloat16), value, preferred_element_type=jnp.float32
             )
-        totals = jnp.sum(summed, axis=1, keepdims=True)
         held[block] = (numer / totals).astype(jnp.bfloat16)
     ids_copy.wait()
     id_rows = jnp.broadcast_to(
@@ -473,7 +473,8 @@
             summed = plus(part, swap(part_across, 2))
             arrived.append(swap(summed, offset))
     part, part_across = mix({0: normed, 2: across})
-    part_beside, part_both = mix({4: beside, 6: beside_across})
+    (part_beside,) = mix({4: beside})
+    (part_both,) = mix({6: beside_across})
     summed = plus(part_across, swap(part_both, 4))
     (result,) = call(
         finish_kernel,

time: 190 us -> 186 us (0.979)
  the two profiles are of different devices: /device:TPU:1 before, /device:TPU:0 now
where the time goes in v1:
time: 186 us
  starting transfers between devices  92 us (49%)
  waiting for transfers between devices  62.2 us (33%)
  Pallas kernels  30.5 us (16%)
    ppermute x41, starting transfers between devices, swap(): lax.ppermute(array, 'ctx', [(i, i ^ mask) for i in range(lax.axis_size('c...  92 us
    ppermute x41, waiting for transfers between devices, swap(): lax.ppermute(array, 'ctx', [(i, i ^ mask) for i in range(lax.axis_size('c...  62.2 us
    pallas_call x13, Pallas kernels, call(): pl.pallas_call(kernel, out_shape=outs, in_specs=specs, out_specs=[VMEM] *...  30.5 us
  transfers between devices with their start and end apart: 41, of which 14 were waited for; matrix products, arithmetic and copies ran while one was open for 0% of the time, Pallas kernels for 15%

profile of v1, /device:TPU:0, one launch (start us, length us, event | category | flops | bytes accessed | tf_op | source)
XLA Modules:
  0.0 186.0 jit_solution(17679322823070710175)
XLA Ops:
  1.3 3.1 %collective-permute-start = (bf16[128,384]{1,0:T(8,128)(2,1)S(1)}, bf16[128,384]{1,0:T(8,128)(2,1)S(1)}, u32[]{:S(2)}, u32[]{:S(2)}) collective-permute-start(bf16[128,384]{1,0:T(8,128)(2,1)S(1)} %get-tuple-element.46), channel_id=1, source_target_pairs={{0,2},{1,3},{2,0},{3,1},{4,6},{5,7},{6,4},{7,5},{8,10},{9,11},{10,... | collective-permute-start | bytes 294920 | tf_op jit(solution)/shard_map/ppermute | solution.py:183
  6.0 3.0 %collective-permute-start.3 = (bf16[128,384]{1,0:T(8,128)(2,1)S(1)}, bf16[128,384]{1,0:T(8,128)(2,1)S(1)}, u32[]{:S(2)}, u32[]{:S(2)}) collective-permute-start(bf16[128,384]{1,0:T(8,128)(2,1)S(1)} %get-tuple-element.49), channel_id=1, source_target_pairs={{0,8},{1,9},{2,10},{3,11},{4,12},{5,13},{6,14},{7,15},{8,0},{9,1},... | collective-permute-start | bytes 294920 | tf_op jit(solution)/shard_map/ppermute | solution.py:183
  10.2 3.6 %collective-permute-start.5 = (bf16[128,384]{1,0:T(8,128)(2,1)S(1)}, bf16[128,384]{1,0:T(8,128)(2,1)S(1)}, u32[]{:S(2)}, u32[]{:S(2)}) collective-permute-start(bf16[128,384]{1,0:T(8,128)(2,1)S(1)} %get-tuple-element.51), channel_id=1, source_target_pairs={{0,12},{1,13},{2,14},{3,15},{4,8},{5,9},{6,10},{7,11},{8,4},{9,5},... | collective-permute-start | bytes 294920 | tf_op jit(solution)/shard_map/ppermute | solution.py:183
  13.9 10.3 %collective-permute-done.4.refs_5_ = bf16[128,384]{1,0:T(8,128)(2,1)S(1)} collective-permute-done((bf16[128,384]{1,0:T(8,128)(2,1)S(1)}, bf16[128,384]{1,0:T(8,128)(2,1)S(1)}, u32[]{:S(2)}, u32[]{:S(2)}) %collective-permute-start.4) | collective-permute-done | bytes 98336 | tf_op jit(solution)/shard_map/ppermute | solution.py:183
  26.9 3.3 %shard_map.121 = (bf16[144,128]{1,0:T(8,128)(2,1)S(1)}, bf16[144,128]{1,0:T(8,128)(2,1)S(1)}, bf16[144,128]{1,0:T(8,128)(2,1)S(1)}, bf16[144,128]{1,0:T(8,128)(2...) custom-call(s32[1]{0:T(128)} %bitcast.index_ref, ...), custom_call_target="tpu_custom_call" | custom-call | flops 1000000000 | bytes 1311236 | tf_op jit(solution)/shard_map/pallas_call | solution.py:194
  31.1 3.6 %collective-permute-start.9 = (bf16[144,128]{1,0:T(8,128)(2,1)S(1)}, bf16[144,128]{1,0:T(8,128)(2,1)S(1)}, u32[]{:S(2)}, u32[]{:S(2)}) collective-permute-start(bf16[144,128]{1,0:T(8,128)(2,1)S(1)} %get-tuple-element.57), channel_id=1, source_target_pairs={{0,4},{1,5},{2,6},{3,7},{4,0},{5,1},{6,2},{7,3},{8,12},{9,13},{10,... | collective-permute-start | bytes 110600 | tf_op jit(solution)/shard_map/ppermute | solution.py:183
  35.7 3.6 %collective-permute-start.11 = (bf16[144,128]{1,0:T(8,128)(2,1)S(1)}, bf16[144,128]{1,0:T(8,128)(2,1)S(1)}, u32[]{:S(2)}, u32[]{:S(2)}) collective-permute-start(bf16[144,128]{1,0:T(8,128)(2,1)S(1)} %get-tuple-element.59), channel_id=1, source_target_pairs={{0,8},{1,9},{2,10},{3,11},{4,12},{5,13},{6,14},{7,15},{8,0},{9,1},... | collective-permute-start | bytes 110600 | tf_op jit(solution)/shard_map/ppermute | solution.py:183
  42.3 2.5 %collective-permute-start.14 = (bf16[144,128]{1,0:T(8,128)(2,1)S(1)}, bf16[144,128]{1,0:T(8,128)(2,1)S(1)}, u32[]{:S(2)}, u32[]{:S(2)}) collective-permute-start(bf16[144,128]{1,0:T(8,128)(2,1)S(1)} %get-tuple-element.62), channel_id=1, source_target_pairs={{0,14},{1,15},{2,12},{3,13},{4,10},{5,11},{6,8},{7,9},{8,6},{9,7},... | collective-permute-start | bytes 110600 | tf_op jit(solution)/shard_map/ppermute | solution.py:183
  44.8 4.2 %shard_map.118 = (bf16[2048,256]{1,0:T(8,128)(2,1)S(1)}, bf16[2048,512]{1,0:T(8,128)(2,1)S(1)}, bf16[2048,256]{1,0:T(8,128)(2,1)S(1)}, bf16[512,2048]{1,0:T(8,12...) custom-call(bf16[2048,256]{1,0:T(8,128)(2,1)} %refs_0_.1, bf16[2048,512]{1,0:T(8,128)(2,1)} %bitcast.16, ...), custom_call_target="tpu_custom_call" | custom-call | bytes 11010048 | tf_op jit(solution)/shard_map/pallas_call | solution.py:194
  50.0 2.5 %collective-permute-start.25 = (bf16[64,2048]{1,0:T(8,128)(2,1)S(1)}, bf16[64,2048]{1,0:T(8,128)(2,1)S(1)}, u32[]{:S(2)}, u32[]{:S(2)}) collective-permute-start(bf16[64,2048]{1,0:T(8,128)(2,1)S(1)} %get-tuple-element.71), channel_id=1, source_target_pairs={{0,12},{1,13},{2,14},{3,15},{4,8},{5,9},{6,10},{7,11},{8,4},{9,5},... | collective-permute-start | bytes 786440 | tf_op jit(solution)/shard_map/ppermute | solution.py:183
  53.8 5.2 %collective-permute-done.25.refs_0_ = bf16[64,2048]{1,0:T(8,128)(2,1)S(1)} collective-permute-done((bf16[64,2048]{1,0:T(8,128)(2,1)S(1)}, bf16[64,2048]{1,0:T(8,128)(2,1)S(1)}, u32[]{:S(2)}, u32[]{:S(2)}) %collective-permute-start.25) | collective-permute-done | bytes 262176 | tf_op jit(solution)/shard_map/ppermute | solution.py:183
  59.1 14.3 %collective-permute-start.33 = (bf16[64,2048]{1,0:T(8,128)(2,1)S(1)}, bf16[64,2048]{1,0:T(8,128)(2,1)S(1)}, u32[]{:S(2)}, u32[]{:S(2)}) collective-permute-start(bf16[64,2048]{1,0:T(8,128)(2,1)S(1)} %get-tuple-element.71), channel_id=1, source_target_pairs={{0,8},{1,9},{2,10},{3,11},{4,12},{5,13},{6,14},{7,15},{8,0},{9,1},... | collective-permute-start | bytes 786440 | tf_op jit(solution)/shard_map/ppermute | solution.py:183
  73.3 11.2 %collective-permute-start.37 = (bf16[64,2048]{1,0:T(8,128)(2,1)S(1)}, bf16[64,2048]{1,0:T(8,128)(2,1)S(1)}, u32[]{:S(2)}, u32[]{:S(2)}) collective-permute-start(bf16[64,2048]{1,0:T(8,128)(2,1)S(1)} %get-tuple-element.74), channel_id=1, source_target_pairs={{0,8},{1,9},{2,10},{3,11},{4,12},{5,13},{6,14},{7,15},{8,0},{9,1},... | collective-permute-start | bytes 786440 | tf_op jit(solution)/shard_map/ppermute | solution.py:183
  84.5 7.0 %collective-permute-done.33.refs_0_ = bf16[64,2048]{1,0:T(8,128)(2,1)S(1)} collective-permute-done((bf16[64,2048]{1,0:T(8,128)(2,1)S(1)}, bf16[64,2048]{1,0:T(8,128)(2,1)S(1)}, u32[]{:S(2)}, u32[]{:S(2)}) %collective-permute-start.33) | collective-permute-done | bytes 262176 | tf_op jit(solution)/shard_map/ppermute | solution.py:183
  91.5 3.0 %collective-permute-done.37.refs_0_ = bf16[64,2048]{1,0:T(8,128)(2,1)S(1)} collective-permute-done((bf16[64,2048]{1,0:T(8,128)(2,1)S(1)}, bf16[64,2048]{1,0:T(8,128)(2,1)S(1)}, u32[]{:S(2)}, u32[]{:S(2)}) %collective-permute-start.37) | collective-permute-done | bytes 262176 | tf_op jit(solution)/shard_map/ppermute | solution.py:183
  96.0 10.6 %collective-permute-done.19.refs_1_ = bf16[128,2048]{1,0:T(8,128)(2,1)S(1)} collective-permute-done((bf16[128,2048]{1,0:T(8,128)(2,1)S(1)}, bf16[128,2048]{1,0:T(8,128)(2,1)S(1)}, u32[]{:S(2)}, u32[]{:S(2)}) %collective-permute-start.19) | collective-permute-done | bytes 524320 | tf_op jit(solution)/shard_map/ppermute | solution.py:183
  109.0 2.0 %collective-permute-start.34 = (bf16[64,2048]{1,0:T(8,128)(2,1)S(1)}, bf16[64,2048]{1,0:T(8,128)(2,1)S(1)}, u32[]{:S(2)}, u32[]{:S(2)}) collective-permute-start(bf16[64,2048]{1,0:T(8,128)(2,1)S(1)} %collective-permute-done.33.refs_0_), channel_id=1, source_target_pairs={{0,2},{1,3},{2,0},{3,1},{4,6},{5,7},{6,4},{7,5},{8,10},{9,11},{10,... | collective-permute-start | bytes 786440 | tf_op jit(solution)/shard_map/ppermute | solution.py:183
  111.1 2.6 %shard_map.124 = bf16[128,2048]{1,0:T(8,128)(2,1)S(1)} custom-call(s32[1]{0:T(128)} %bitcast.index_ref, bf16[2,2048]{1,0:T(2,128)(2,1)S(1)} %bitcast.6, bf16[2048,256]{1,0:T(8,128)(2,1)S(1)} %get-tuple-element.64.up_a, bf16[2048,256]{1,0:T(8,128)(2,1)S(1)} %collective-permute-done.15.up_b, bf16[2048,512]{1,0:T(8,128)(2,1)S(1)} %get-tuple-element.65.in_a, ...), custom_call_target="tpu_custom_call" | custom-call | flops 1610612736 | bytes 13152260 | tf_op jit(solution)/shard_map/pallas_call | solution.py:194
  113.7 5.0 %collective-permute-done.22.refs_0_ = bf16[128,2048]{1,0:T(8,128)(2,1)S(1)} collective-permute-done((bf16[128,2048]{1,0:T(8,128)(2,1)S(1)}, bf16[128,2048]{1,0:T(8,128)(2,1)S(1)}, u32[]{:S(2)}, u32[]{:S(2)}) %collective-permute-start.22) | collective-permute-done | bytes 524320 | tf_op jit(solution)/shard_map/ppermute | solution.py:183
  118.7 2.6 %shard_map.125 = bf16[128,2048]{1,0:T(8,128)(2,1)S(1)} custom-call(s32[1]{0:T(128)} %bitcast.index_ref, bf16[2,2048]{1,0:T(2,128)(2,1)S(1)} %bitcast.7, bf16[2048,256]{1,0:T(8,128)(2,1)S(1)} %get-tuple-element.64.up_a, bf16[2048,256]{1,0:T(8,128)(2,1)S(1)} %collective-permute-done.15.up_b, bf16[2048,512]{1,0:T(8,128)(2,1)S(1)} %get-tuple-element.65.in_a, ...), custom_call_target="tpu_custom_call" | custom-call | flops 1610612736 | bytes 13152260 | tf_op jit(solution)/shard_map/pallas_call | solution.py:194
  121.3 2.1 %collective-permute-start.23 = (bf16[128,2048]{1,0:T(8,128)(2,1)S(1)}, bf16[128,2048]{1,0:T(8,128)(2,1)S(1)}, u32[]{:S(2)}, u32[]{:S(2)}) collective-permute-start(bf16[128,2048]{1,0:T(8,128)(2,1)S(1)} %shard_map.125), channel_id=1, source_target_pairs={{0,4},{1,5},{2,6},{3,7},{4,0},{5,1},{6,2},{7,3},{8,12},{9,13},{10,... | collective-permute-start | bytes 1572872 | tf_op jit(solution)/shard_map/ppermute | solution.py:183
  123.4 2.7 %shard_map.126 = (bf16[64,2048]{1,0:T(8,128)(2,1)S(1)}, bf16[64,2048]{1,0:T(8,128)(2,1)S(1)}) custom-call(s32[1]{0:T(128)} %bitcast.index_ref, bf16[2,2048]{1,0:T(2,128)(2,1)S(1)} %bitcast.8, bf16[2048,256]{1,0:T(8,128)(2,1)S(1)} %get-tuple-element.64.up_a, bf16[2048,256]{1,0:T(8,128)(2,1)S(1)} %collective-permute-done.15.up_b, ...), custom_call_target="tpu_custom_call" | custom-call | flops 1610612736 | bytes 13189124 | tf_op jit(solution)/shard_map/pallas_call | solution.py:194
  127.7 2.6 %shard_map.127 = (bf16[64,2048]{1,0:T(8,128)(2,1)S(1)}, bf16[64,2048]{1,0:T(8,128)(2,1)S(1)}) custom-call(s32[1]{0:T(128)} %bitcast.index_ref, bf16[2,2048]{1,0:T(2,128)(2,1)S(1)} %bitcast.9, bf16[2048,256]{1,0:T(8,128)(2,1)S(1)} %get-tuple-element.64.up_a, bf16[2048,256]{1,0:T(8,128)(2,1)S(1)} %collective-permute-done.15.up_b, ...), custom_call_target="tpu_custom_call" | custom-call | flops 1610612736 | bytes 13189124 | tf_op jit(solution)/shard_map/pallas_call | solution.py:194
  130.9 2.6 %shard_map.128 = (bf16[64,2048]{1,0:T(8,128)(2,1)S(1)}, bf16[64,2048]{1,0:T(8,128)(2,1)S(1)}) custom-call(s32[1]{0:T(128)} %bitcast.index_ref, bf16[2,2048]{1,0:T(2,128)(2,1)S(1)} %bitcast.10, bf16[2048,256]{1,0:T(8,128)(2,1)S(1)} %get-tuple-element.64.up_a, bf16[2048,256]{1,0:T(8,128)(2,1)S(1)} %collective-permute-done.15.up_b, ...), custom_call_target="tpu_custom_call" | custom-call | flops 1610612736 | bytes 13189124 | tf_op jit(solution)/shard_map/pallas_call | solution.py:194
  135.0 2.6 %shard_map.129 = (bf16[64,2048]{1,0:T(8,128)(2,1)S(1)}, bf16[64,2048]{1,0:T(8,128)(2,1)S(1)}) custom-call(s32[1]{0:T(128)} %bitcast.index_ref, bf16[2,2048]{1,0:T(2,128)(2,1)S(1)} %bitcast.11, bf16[2048,256]{1,0:T(8,128)(2,1)S(1)} %get-tuple-element.64.up_a, bf16[2048,256]{1,0:T(8,128)(2,1)S(1)} %collective-permute-done.15.up_b, ...), custom_call_target="tpu_custom_call" | custom-call | flops 1610612736 | bytes 13189124 | tf_op jit(solution)/shard_map/pallas_call | solution.py:194
  137.6 3.9 %shard_map.123 = (bf16[128,2048]{1,0:T(8,128)(2,1)S(1)}, bf16[128,2048]{1,0:T(8,128)(2,1)S(1)}) custom-call(s32[1]{0:T(128)} %bitcast.index_ref, bf16[2,2048]{1,0:T(2,128)(2,1)S(1)} %bitcast.12, bf16[2048,256]{1,0:T(8,128)(2,1)S(1)} %get-tuple-element.64.up_a, bf16[2048,256]{1,0:T(8,128)(2,1)S(1)} %collective-permute-done.15.up_b, ...), custom_call_target="tpu_custom_call" | custom-call | flops 3221225472 | bytes 13713412 | tf_op jit(solution)/shard_map/pallas_call | solution.py:194
  143.0 3.0 %collective-permute-start.28 = (bf16[64,2048]{1,0:T(8,128)(2,1)S(1)}, bf16[64,2048]{1,0:T(8,128)(2,1)S(1)}, u32[]{:S(2)}, u32[]{:S(2)}) collective-permute-start(bf16[64,2048]{1,0:T(8,128)(2,1)S(1)} %add_convert_fusion.4), channel_id=1, source_target_pairs={{0,12},{1,13},{2,14},{3,15},{4,8},{5,9},{6,10},{7,11},{8,4},{9,5},... | collective-permute-start | bytes 786440 | tf_op jit(solution)/shard_map/ppermute | solution.py:183
  148.0 2.4 %collective-permute-start.32 = (bf16[64,2048]{1,0:T(8,128)(2,1)S(1)}, bf16[64,2048]{1,0:T(8,128)(2,1)S(1)}, u32[]{:S(2)}, u32[]{:S(2)}) collective-permute-start(bf16[64,2048]{1,0:T(8,128)(2,1)S(1)} %add_convert_fusion.3), channel_id=1, source_target_pairs={{0,12},{1,13},{2,14},{3,15},{4,8},{5,9},{6,10},{7,11},{8,4},{9,5},... | collective-permute-start | bytes 786440 | tf_op jit(solution)/shard_map/ppermute | solution.py:183
  151.6 2.3 %collective-permute-start.24 = (bf16[128,2048]{1,0:T(8,128)(2,1)S(1)}, bf16[128,2048]{1,0:T(8,128)(2,1)S(1)}, u32[]{:S(2)}, u32[]{:S(2)}) collective-permute-start(bf16[128,2048]{1,0:T(8,128)(2,1)S(1)} %add_convert_fusion), channel_id=1, source_target_pairs={{0,2},{1,3},{2,0},{3,1},{4,6},{5,7},{6,4},{7,5},{8,10},{9,11},{10,... | collective-permute-start | bytes 1572872 | tf_op jit(solution)/shard_map/ppermute | solution.py:183
  154.1 15.5 %collective-permute-start.40 = (bf16[64,2048]{1,0:T(8,128)(2,1)S(1)}, bf16[64,2048]{1,0:T(8,128)(2,1)S(1)}, u32[]{:S(2)}, u32[]{:S(2)}) collective-permute-start(bf16[64,2048]{1,0:T(8,128)(2,1)S(1)} %add_convert_fusion.1), channel_id=1, source_target_pairs={{0,8},{1,9},{2,10},{3,11},{4,12},{5,13},{6,14},{7,15},{8,0},{9,1},... | collective-permute-start | bytes 786440 | tf_op jit(solution)/shard_map/ppermute | solution.py:183
  169.6 12.4 %collective-permute-done.36.refs_5_ = bf16[64,2048]{1,0:T(8,128)(2,1)S(1)} collective-permute-done((bf16[64,2048]{1,0:T(8,128)(2,1)S(1)}, bf16[64,2048]{1,0:T(8,128)(2,1)S(1)}, u32[]{:S(2)}, u32[]{:S(2)}) %collective-permute-start.36) | collective-permute-done | bytes 262176 | tf_op jit(solution)/shard_map/ppermute | solution.py:183
  182.0 2.8 %collective-permute-done.40.refs_6_ = bf16[64,2048]{1,0:T(8,128)(2,1)S(1)} collective-permute-done((bf16[64,2048]{1,0:T(8,128)(2,1)S(1)}, bf16[64,2048]{1,0:T(8,128)(2,1)S(1)}, u32[]{:S(2)}, u32[]{:S(2)}) %collective-permute-start.40) | collective-permute-done | bytes 262176 | tf_op jit(solution)/shard_map/ppermute | solution.py:183
  (78 shorter events, 27.7 us)
Async XLA Ops:
  1.3 8.9 %collective-permute-start = (bf16[128,384]{1,0:T(8,128)(2,1)S(1)}, bf16[128,384]{1,0:T(8,128)(2,1)S(1)}, u32[]{:S(2)}, u32[]{:S(2)}) collective-permute-start(bf16[128,384]{1,0:T(8,128)(2,1)S(1)} %get-tuple-element.46), channel_id=1, source_target_pairs={{0,2},{1,3},{2,0},{3,1},{4,6},{5,7},{6,4},{7,5},{8,10},{9,11},{10,... | collective-permute-start | bytes 294920 | tf_op jit(solution)/shard_map/ppermute | solution.py:183
  4.4 9.5 %collective-permute-start.1 = (bf16[128,384]{1,0:T(8,128)(2,1)S(1)}, bf16[128,384]{1,0:T(8,128)(2,1)S(1)}, u32[]{:S(2)}, u32[]{:S(2)}) collective-permute-start(bf16[128,384]{1,0:T(8,128)(2,1)S(1)} %get-tuple-element.47), channel_id=1, source_target_pairs={{0,4},{1,5},{2,6},{3,7},{4,0},{5,1},{6,2},{7,3},{8,12},{9,13},{10,... | collective-permute-start | bytes 294920 | tf_op jit(solution)/shard_map/ppermute | solution.py:183
  8.9 15.2 %collective-permute-start.4 = (bf16[128,384]{1,0:T(8,128)(2,1)S(1)}, bf16[128,384]{1,0:T(8,128)(2,1)S(1)}, u32[]{:S(2)}, u32[]{:S(2)}) collective-permute-start(bf16[128,384]{1,0:T(8,128)(2,1)S(1)} %get-tuple-element.50), channel_id=1, source_target_pairs={{0,10},{1,11},{2,8},{3,9},{4,14},{5,15},{6,12},{7,13},{8,2},{9,3},... | collective-permute-start | bytes 294920 | tf_op jit(solution)/shard_map/ppermute | solution.py:183
  10.2 13.9 %collective-permute-start.5 = (bf16[128,384]{1,0:T(8,128)(2,1)S(1)}, bf16[128,384]{1,0:T(8,128)(2,1)S(1)}, u32[]{:S(2)}, u32[]{:S(2)}) collective-permute-start(bf16[128,384]{1,0:T(8,128)(2,1)S(1)} %get-tuple-element.51), channel_id=1, source_target_pairs={{0,12},{1,13},{2,14},{3,15},{4,8},{5,9},{6,10},{7,11},{8,4},{9,5},... | collective-permute-start | bytes 294920 | tf_op jit(solution)/shard_map/ppermute | solution.py:183
  13.8 10.3 %collective-permute-start.6 = (bf16[128,384]{1,0:T(8,128)(2,1)S(1)}, bf16[128,384]{1,0:T(8,128)(2,1)S(1)}, u32[]{:S(2)}, u32[]{:S(2)}) collective-permute-start(bf16[128,384]{1,0:T(8,128)(2,1)S(1)} %get-tuple-element.52), channel_id=1, source_target_pairs={{0,14},{1,15},{2,12},{3,13},{4,10},{5,11},{6,8},{7,9},{8,6},{9,7},... | collective-permute-start | bytes 294920 | tf_op jit(solution)/shard_map/ppermute | solution.py:183
  24.3 84.7 %collective-permute-start.16 = (bf16[2048,512]{1,0:T(8,128)(2,1)}, bf16[2048,512]{1,0:T(8,128)(2,1)S(1)}, u32[]{:S(2)}, u32[]{:S(2)}) collective-permute-start(bf16[2048,512]{1,0:T(8,128)(2,1)} %bitcast.15), channel_id=1, source_target_pairs={{0,1},{1,0},{2,3},{3,2},{4,5},{5,4},{6,7},{7,6},{8,9},{9,8},{10,11... | collective-permute-start | bytes 6291464 | tf_op jit(solution)/shard_map/ppermute | solution.py:183
  24.8 86.2 %collective-permute-start.18 = (bf16[512,2048]{1,0:T(8,128)(2,1)}, bf16[512,2048]{1,0:T(8,128)(2,1)S(1)}, u32[]{:S(2)}, u32[]{:S(2)}) collective-permute-start(bf16[512,2048]{1,0:T(8,128)(2,1)} %bitcast.17), channel_id=1, source_target_pairs={{0,1},{1,0},{2,3},{3,2},{4,5},{5,4},{6,7},{7,6},{8,9},{9,8},{10,11... | collective-permute-start | bytes 6291464 | tf_op jit(solution)/shard_map/ppermute | solution.py:183
  39.3 9.7 %collective-permute-start.12 = (bf16[144,128]{1,0:T(8,128)(2,1)S(1)}, bf16[144,128]{1,0:T(8,128)(2,1)S(1)}, u32[]{:S(2)}, u32[]{:S(2)}) collective-permute-start(bf16[144,128]{1,0:T(8,128)(2,1)S(1)} %get-tuple-element.60), channel_id=1, source_target_pairs={{0,10},{1,11},{2,8},{3,9},{4,14},{5,15},{6,12},{7,13},{8,2},{9,3},... | collective-permute-start | bytes 110600 | tf_op jit(solution)/shard_map/ppermute | solution.py:183
  50.0 9.1 %collective-permute-start.25 = (bf16[64,2048]{1,0:T(8,128)(2,1)S(1)}, bf16[64,2048]{1,0:T(8,128)(2,1)S(1)}, u32[]{:S(2)}, u32[]{:S(2)}) collective-permute-start(bf16[64,2048]{1,0:T(8,128)(2,1)S(1)} %get-tuple-element.71), channel_id=1, source_target_pairs={{0,12},{1,13},{2,14},{3,15},{4,8},{5,9},{6,10},{7,11},{8,4},{9,5},... | collective-permute-start | bytes 786440 | tf_op jit(solution)/shard_map/ppermute | solution.py:183
  52.4 43.6 %collective-permute-start.15 = (bf16[2048,256]{1,0:T(8,128)(2,1)S(1)}, bf16[2048,256]{1,0:T(8,128)(2,1)S(1)}, u32[]{:S(2)}, u32[]{:S(2)}) collective-permute-start(bf16[2048,256]{1,0:T(8,128)(2,1)S(1)} %copy-done.3), channel_id=1, source_target_pairs={{0,1},{1,0},{2,3},{3,2},{4,5},{5,4},{6,7},{7,6},{8,9},{9,8},{10,11... | collective-permute-start | bytes 3145736 | tf_op jit(solution)/shard_map/ppermute | solution.py:183
  52.4 20.9 %collective-permute-start.29 = (bf16[64,2048]{1,0:T(8,128)(2,1)S(1)}, bf16[64,2048]{1,0:T(8,128)(2,1)S(1)}, u32[]{:S(2)}, u32[]{:S(2)}) collective-permute-start(bf16[64,2048]{1,0:T(8,128)(2,1)S(1)} %get-tuple-element.74), channel_id=1, source_target_pairs={{0,12},{1,13},{2,14},{3,15},{4,8},{5,9},{6,10},{7,11},{8,4},{9,5},... | collective-permute-start | bytes 786440 | tf_op jit(solution)/shard_map/ppermute | solution.py:183
  59.1 32.4 %collective-permute-start.33 = (bf16[64,2048]{1,0:T(8,128)(2,1)S(1)}, bf16[64,2048]{1,0:T(8,128)(2,1)S(1)}, u32[]{:S(2)}, u32[]{:S(2)}) collective-permute-start(bf16[64,2048]{1,0:T(8,128)(2,1)S(1)} %get-tuple-element.71), channel_id=1, source_target_pairs={{0,8},{1,9},{2,10},{3,11},{4,12},{5,13},{6,14},{7,15},{8,0},{9,1},... | collective-permute-start | bytes 786440 | tf_op jit(solution)/shard_map/ppermute | solution.py:183
  73.3 21.2 %collective-permute-start.37 = (bf16[64,2048]{1,0:T(8,128)(2,1)S(1)}, bf16[64,2048]{1,0:T(8,128)(2,1)S(1)}, u32[]{:S(2)}, u32[]{:S(2)}) collective-permute-start(bf16[64,2048]{1,0:T(8,128)(2,1)S(1)} %get-tuple-element.74), channel_id=1, source_target_pairs={{0,8},{1,9},{2,10},{3,11},{4,12},{5,13},{6,14},{7,15},{8,0},{9,1},... | collective-permute-start | bytes 786440 | tf_op jit(solution)/shard_map/ppermute | solution.py:183
  91.5 15.1 %collective-permute-start.17 = (bf16[2048,256]{1,0:T(8,128)(2,1)S(1)}, bf16[2048,256]{1,0:T(8,128)(2,1)S(1)}, u32[]{:S(2)}, u32[]{:S(2)}) collective-permute-start(bf16[2048,256]{1,0:T(8,128)(2,1)S(1)} %copy-done.4), channel_id=1, source_target_pairs={{0,1},{1,0},{2,3},{3,2},{4,5},{5,4},{6,7},{7,6},{8,9},{9,8},{10,11... | collective-permute-start | bytes 3145736 | tf_op jit(solution)/shard_map/ppermute | solution.py:183
  94.5 12.1 %collective-permute-start.19 = (bf16[128,2048]{1,0:T(8,128)(2,1)S(1)}, bf16[128,2048]{1,0:T(8,128)(2,1)S(1)}, u32[]{:S(2)}, u32[]{:S(2)}) collective-permute-start(bf16[128,2048]{1,0:T(8,128)(2,1)S(1)} %get-tuple-element.68.refs_0_), channel_id=1, source_target_pairs={{0,2},{1,3},{2,0},{3,1},{4,6},{5,7},{6,4},{7,5},{8,10},{9,11},{10,... | collective-permute-start | bytes 1572872 | tf_op jit(solution)/shard_map/ppermute | solution.py:183
  96.0 13.0 %collective-permute-start.20 = (bf16[128,2048]{1,0:T(8,128)(2,1)S(1)}, bf16[128,2048]{1,0:T(8,128)(2,1)S(1)}, u32[]{:S(2)}, u32[]{:S(2)}) collective-permute-start(bf16[128,2048]{1,0:T(8,128)(2,1)S(1)} %get-tuple-element.68.refs_0_), channel_id=1, source_target_pairs={{0,4},{1,5},{2,6},{3,7},{4,0},{5,1},{6,2},{7,3},{8,12},{9,13},{10,... | collective-permute-start | bytes 1572872 | tf_op jit(solution)/shard_map/ppermute | solution.py:183
  106.6 12.1 %collective-permute-start.22 = (bf16[128,2048]{1,0:T(8,128)(2,1)S(1)}, bf16[128,2048]{1,0:T(8,128)(2,1)S(1)}, u32[]{:S(2)}, u32[]{:S(2)}) collective-permute-start(bf16[128,2048]{1,0:T(8,128)(2,1)S(1)} %collective-permute-done.19.refs_1_), channel_id=1, source_target_pairs={{0,4},{1,5},{2,6},{3,7},{4,0},{5,1},{6,2},{7,3},{8,12},{9,13},{10,... | collective-permute-start | bytes 1572872 | tf_op jit(solution)/shard_map/ppermute | solution.py:183
  106.6 14.7 %collective-permute-start.26 = (bf16[64,2048]{1,0:T(8,128)(2,1)S(1)}, bf16[64,2048]{1,0:T(8,128)(2,1)S(1)}, u32[]{:S(2)}, u32[]{:S(2)}) collective-permute-start(bf16[64,2048]{1,0:T(8,128)(2,1)S(1)} %collective-permute-done.25.refs_0_), channel_id=1, source_target_pairs={{0,2},{1,3},{2,0},{3,1},{4,6},{5,7},{6,4},{7,5},{8,10},{9,11},{10,... | collective-permute-start | bytes 786440 | tf_op jit(solution)/shard_map/ppermute | solution.py:183
  109.0 17.1 %collective-permute-start.30 = (bf16[64,2048]{1,0:T(8,128)(2,1)S(1)}, bf16[64,2048]{1,0:T(8,128)(2,1)S(1)}, u32[]{:S(2)}, u32[]{:S(2)}) collective-permute-start(bf16[64,2048]{1,0:T(8,128)(2,1)S(1)} %collective-permute-done.29.refs_0_), channel_id=1, source_target_pairs={{0,2},{1,3},{2,0},{3,1},{4,6},{5,7},{6,4},{7,5},{8,10},{9,11},{10,... | collective-permute-start | bytes 786440 | tf_op jit(solution)/shard_map/ppermute | solution.py:183
  109.0 21.2 %collective-permute-start.34 = (bf16[64,2048]{1,0:T(8,128)(2,1)S(1)}, bf16[64,2048]{1,0:T(8,128)(2,1)S(1)}, u32[]{:S(2)}, u32[]{:S(2)}) collective-permute-start(bf16[64,2048]{1,0:T(8,128)(2,1)S(1)} %collective-permute-done.33.refs_0_), channel_id=1, source_target_pairs={{0,2},{1,3},{2,0},{3,1},{4,6},{5,7},{6,4},{7,5},{8,10},{9,11},{10,... | collective-permute-start | bytes 786440 | tf_op jit(solution)/shard_map/ppermute | solution.py:183
  111.0 22.4 %collective-permute-start.38 = (bf16[64,2048]{1,0:T(8,128)(2,1)S(1)}, bf16[64,2048]{1,0:T(8,128)(2,1)S(1)}, u32[]{:S(2)}, u32[]{:S(2)}) collective-permute-start(bf16[64,2048]{1,0:T(8,128)(2,1)S(1)} %collective-permute-done.37.refs_0_), channel_id=1, source_target_pairs={{0,2},{1,3},{2,0},{3,1},{4,6},{5,7},{6,4},{7,5},{8,10},{9,11},{10,... | collective-permute-start | bytes 786440 | tf_op jit(solution)/shard_map/ppermute | solution.py:183
  118.7 66.1 %collective-permute-start.21 = (bf16[128,2048]{1,0:T(8,128)(2,1)S(1)}, bf16[128,2048]{1,0:T(8,128)(2,1)S(1)}, u32[]{:S(2)}, u32[]{:S(2)}) collective-permute-start(bf16[128,2048]{1,0:T(8,128)(2,1)S(1)} %shard_map.124), channel_id=1, source_target_pairs={{0,4},{1,5},{2,6},{3,7},{4,0},{5,1},{6,2},{7,3},{8,12},{9,13},{10,... | collective-permute-start | bytes 1572872 | tf_op jit(solution)/shard_map/ppermute | solution.py:183
  121.3 29.2 %collective-permute-start.23 = (bf16[128,2048]{1,0:T(8,128)(2,1)S(1)}, bf16[128,2048]{1,0:T(8,128)(2,1)S(1)}, u32[]{:S(2)}, u32[]{:S(2)}) collective-permute-start(bf16[128,2048]{1,0:T(8,128)(2,1)S(1)} %shard_map.125), channel_id=1, source_target_pairs={{0,4},{1,5},{2,6},{3,7},{4,0},{5,1},{6,2},{7,3},{8,12},{9,13},{10,... | collective-permute-start | bytes 1572872 | tf_op jit(solution)/shard_map/ppermute | solution.py:183
  126.1 15.4 %collective-permute-start.27 = (bf16[64,2048]{1,0:T(8,128)(2,1)S(1)}, bf16[64,2048]{1,0:T(8,128)(2,1)S(1)}, u32[]{:S(2)}, u32[]{:S(2)}) collective-permute-start(bf16[64,2048]{1,0:T(8,128)(2,1)S(1)} %get-tuple-element.73), channel_id=1, source_target_pairs={{0,2},{1,3},{2,0},{3,1},{4,6},{5,7},{6,4},{7,5},{8,10},{9,11},{10,... | collective-permute-start | bytes 786440 | tf_op jit(solution)/shard_map/ppermute | solution.py:183
  130.3 12.8 %collective-permute-start.31 = (bf16[64,2048]{1,0:T(8,128)(2,1)S(1)}, bf16[64,2048]{1,0:T(8,128)(2,1)S(1)}, u32[]{:S(2)}, u32[]{:S(2)}) collective-permute-start(bf16[64,2048]{1,0:T(8,128)(2,1)S(1)} %get-tuple-element.76), channel_id=1, source_target_pairs={{0,2},{1,3},{2,0},{3,1},{4,6},{5,7},{6,4},{7,5},{8,10},{9,11},{10,... | collective-permute-start | bytes 786440 | tf_op jit(solution)/shard_map/ppermute | solution.py:183
  133.5 14.5 %collective-permute-start.35 = (bf16[64,2048]{1,0:T(8,128)(2,1)S(1)}, bf16[64,2048]{1,0:T(8,128)(2,1)S(1)}, u32[]{:S(2)}, u32[]{:S(2)}) collective-permute-start(bf16[64,2048]{1,0:T(8,128)(2,1)S(1)} %get-tuple-element.78), channel_id=1, source_target_pairs={{0,2},{1,3},{2,0},{3,1},{4,6},{5,7},{6,4},{7,5},{8,10},{9,11},{10,... | collective-permute-start | bytes 786440 | tf_op jit(solution)/shard_map/ppermute | solution.py:183
  141.6 10.0 %collective-permute-start.39 = (bf16[64,2048]{1,0:T(8,128)(2,1)S(1)}, bf16[64,2048]{1,0:T(8,128)(2,1)S(1)}, u32[]{:S(2)}, u32[]{:S(2)}) collective-permute-start(bf16[64,2048]{1,0:T(8,128)(2,1)S(1)} %get-tuple-element.80), channel_id=1, source_target_pairs={{0,2},{1,3},{2,0},{3,1},{4,6},{5,7},{6,4},{7,5},{8,10},{9,11},{10,... | collective-permute-start | bytes 786440 | tf_op jit(solution)/shard_map/ppermute | solution.py:183
  143.0 11.0 %collective-permute-start.28 = (bf16[64,2048]{1,0:T(8,128)(2,1)S(1)}, bf16[64,2048]{1,0:T(8,128)(2,1)S(1)}, u32[]{:S(2)}, u32[]{:S(2)}) collective-permute-start(bf16[64,2048]{1,0:T(8,128)(2,1)S(1)} %add_convert_fusion.4), channel_id=1, source_target_pairs={{0,12},{1,13},{2,14},{3,15},{4,8},{5,9},{6,10},{7,11},{8,4},{9,5},... | collective-permute-start | bytes 786440 | tf_op jit(solution)/shard_map/ppermute | solution.py:183
  148.0 21.6 %collective-permute-start.32 = (bf16[64,2048]{1,0:T(8,128)(2,1)S(1)}, bf16[64,2048]{1,0:T(8,128)(2,1)S(1)}, u32[]{:S(2)}, u32[]{:S(2)}) collective-permute-start(bf16[64,2048]{1,0:T(8,128)(2,1)S(1)} %add_convert_fusion.3), channel_id=1, source_target_pairs={{0,12},{1,13},{2,14},{3,15},{4,8},{5,9},{6,10},{7,11},{8,4},{9,5},... | collective-permute-start | bytes 786440 | tf_op jit(solution)/shard_map/ppermute | solution.py:183
  150.4 31.6 %collective-permute-start.36 = (bf16[64,2048]{1,0:T(8,128)(2,1)S(1)}, bf16[64,2048]{1,0:T(8,128)(2,1)S(1)}, u32[]{:S(2)}, u32[]{:S(2)}) collective-permute-start(bf16[64,2048]{1,0:T(8,128)(2,1)S(1)} %add_convert_fusion.2), channel_id=1, source_target_pairs={{0,8},{1,9},{2,10},{3,11},{4,12},{5,13},{6,14},{7,15},{8,0},{9,1},... | collective-permute-start | bytes 786440 | tf_op jit(solution)/shard_map/ppermute | solution.py:183
  151.6 33.2 %collective-permute-start.24 = (bf16[128,2048]{1,0:T(8,128)(2,1)S(1)}, bf16[128,2048]{1,0:T(8,128)(2,1)S(1)}, u32[]{:S(2)}, u32[]{:S(2)}) collective-permute-start(bf16[128,2048]{1,0:T(8,128)(2,1)S(1)} %add_convert_fusion), channel_id=1, source_target_pairs={{0,2},{1,3},{2,0},{3,1},{4,6},{5,7},{6,4},{7,5},{8,10},{9,11},{10,... | collective-permute-start | bytes 1572872 | tf_op jit(solution)/shard_map/ppermute | solution.py:183
  154.1 30.7 %collective-permute-start.40 = (bf16[64,2048]{1,0:T(8,128)(2,1)S(1)}, bf16[64,2048]{1,0:T(8,128)(2,1)S(1)}, u32[]{:S(2)}, u32[]{:S(2)}) collective-permute-start(bf16[64,2048]{1,0:T(8,128)(2,1)S(1)} %add_convert_fusion.1), channel_id=1, source_target_pairs={{0,8},{1,9},{2,10},{3,11},{4,12},{5,13},{6,14},{7,15},{8,0},{9,1},... | collective-permute-start | bytes 786440 | tf_op jit(solution)/shard_map/ppermute | solution.py:183
  (14 other events, 174.4 us)

commit v2 on v1

--- a/solution.py
+++ b/solution.py
@@ -179,8 +179,9 @@
 LOG2_E = 1.4426950408889634
 
 
-def swap(array, mask):
-    return lax.ppermute(array, "ctx", [(i, i ^ mask) for i in range(lax.axis_size("ctx"))])
+def swap(array, mask, among=lambda at: True):
+    pairs = [(i, i ^ mask) for i in range(lax.axis_size("ctx")) if among(i)]
+    return lax.ppermute(array, "ctx", pairs)
 
 
 VMEM = pl.BlockSpec(memory_space=pltpu.VMEM)
@@ -379,7 +380,6 @@
 ):
     rows, width = resid.shape
     heads = queries.shape[1] // DH
-    ctx_count = lax.axis_size("ctx")
     device_index = lax.axis_index("ctx")
     index = device_index.reshape(1)
     shape = jax.ShapeDtypeStruct
@@ -456,22 +456,33 @@
             *(backs[offset // 2] for offset in shards),
         )
 
-    def plus(first, second):
-        return (first.astype(jnp.float32) + second.astype(jnp.float32)).astype(jnp.bfloat16)
-
-    far = [4 * at for at in range(ctx_count // 4 - 1, 1, -1)]
+    def plus(*terms):
+        return sum(term.astype(jnp.float32) for term in terms).astype(jnp.bfloat16)
+
+    def inner(at):
+        return (at >> 2 ^ at >> 3) & 1 == 1
+
+    def outer(at):
+        return not inner(at)
+
     across = swap(normed, 2)
     beside = swap(normed, 4)
     beside_across = swap(across, 4)
-    arrived = []
-    for offset in far:
+    arrived, passed = [], {}
+    for offset in (12, 8):
         for half, rows_sent in zip("ab", halves):
             first = swap(rows_sent, offset)
             second = swap(first, 2)
             start = 0 if half == "a" else rows // 2
             part, part_across = mix({offset: first, offset | 2: second}, start)
-            summed = plus(part, swap(part_across, 2))
-            arrived.append(swap(summed, offset))
+            returned = swap(part_across, 2)
+            if offset == 12:
+                summed = plus(part, returned)
+                arrived.append(swap(summed, 12, inner))
+                passed[half] = swap(summed, 4, outer)
+            else:
+                summed = plus(part, returned, passed[half])
+                arrived.append(swap(summed, 8))
     part, part_across = mix({0: normed, 2: across})
     (part_beside,) = mix({4: beside})
     (part_both,) = mix({6: beside_across})
@@ -500,8 +511,7 @@
             router.shape[1] == 2
             and ctx_count == 2 * SPLIT
             and queries.shape[1] == ctx_count // 2 * DH
-            and ctx_count % 4 == 0
-            and ctx_count & (ctx_count - 1) == 0
+            and ctx_count == 16
         )
 
     def chosen(*args):

time: 186 us -> 199 us (1.070)
  waiting for transfers between devices: 62.2 us -> 91.5 us
  starting transfers between devices: 92 us -> 74.8 us
    ppermute x41 -> x43, waiting for transfers between devices: 62.2 us -> 91.5 us  [swap(): return lax.ppermute(array, 'ctx', pairs)]
    ppermute x41 -> x43, starting transfers between devices: 92 us -> 74.8 us  [swap(): return lax.ppermute(array, 'ctx', pairs)]
  transfers between devices with their start and end apart: 41 -> 43, of which waited for: 14 -> 13; matrix products, arithmetic and copies ran while one was open for 0% -> 0% of each run, Pallas kernels for 15% -> 14%
where the time goes in v2:
time: 199 us; the launch traced here: 198 us
  waiting for transfers between devices  91.5 us (46%)
  starting transfers between devices  74.8 us (38%)
  Pallas kernels  30.5 us (15%)
    ppermute x43, waiting for transfers between devices, swap(): return lax.ppermute(array, 'ctx', pairs)  91.5 us
    ppermute x43, starting transfers between devices, swap(): return lax.ppermute(array, 'ctx', pairs)  74.8 us
    pallas_call x13, Pallas kernels, call(): pl.pallas_call(kernel, out_shape=outs, in_specs=specs, out_specs=[VMEM] *...  30.5 us
  transfers between devices with their start and end apart: 43, of which 13 were waited for; matrix products, arithmetic and copies ran while one was open for 0% of the time, Pallas kernels for 14%

profile of v2, /device:TPU:0, one launch (start us, length us, event | category | flops | bytes accessed | tf_op | source)
XLA Modules:
  0.0 198.3 jit_solution(4363837979799010045)
XLA Ops:
  1.3 3.1 %collective-permute-start = (bf16[128,384]{1,0:T(8,128)(2,1)S(1)}, bf16[128,384]{1,0:T(8,128)(2,1)S(1)}, u32[]{:S(2)}, u32[]{:S(2)}) collective-permute-start(bf16[128,384]{1,0:T(8,128)(2,1)S(1)} %get-tuple-element.46), channel_id=1, source_target_pairs={{0,2},{1,3},{2,0},{3,1},{4,6},{5,7},{6,4},{7,5},{8,10},{9,11},{10,... | collective-permute-start | bytes 294920 | tf_op jit(solution)/shard_map/ppermute | solution.py:184
  6.0 3.0 %collective-permute-start.3 = (bf16[128,384]{1,0:T(8,128)(2,1)S(1)}, bf16[128,384]{1,0:T(8,128)(2,1)S(1)}, u32[]{:S(2)}, u32[]{:S(2)}) collective-permute-start(bf16[128,384]{1,0:T(8,128)(2,1)S(1)} %get-tuple-element.49), channel_id=1, source_target_pairs={{0,8},{1,9},{2,10},{3,11},{4,12},{5,13},{6,14},{7,15},{8,0},{9,1},... | collective-permute-start | bytes 294920 | tf_op jit(solution)/shard_map/ppermute | solution.py:184
  10.2 3.6 %collective-permute-start.5 = (bf16[128,384]{1,0:T(8,128)(2,1)S(1)}, bf16[128,384]{1,0:T(8,128)(2,1)S(1)}, u32[]{:S(2)}, u32[]{:S(2)}) collective-permute-start(bf16[128,384]{1,0:T(8,128)(2,1)S(1)} %get-tuple-element.51), channel_id=1, source_target_pairs={{0,12},{1,13},{2,14},{3,15},{4,8},{5,9},{6,10},{7,11},{8,4},{9,5},... | collective-permute-start | bytes 294920 | tf_op jit(solution)/shard_map/ppermute | solution.py:184
  13.9 10.3 %collective-permute-done.4.refs_5_ = bf16[128,384]{1,0:T(8,128)(2,1)S(1)} collective-permute-done((bf16[128,384]{1,0:T(8,128)(2,1)S(1)}, bf16[128,384]{1,0:T(8,128)(2,1)S(1)}, u32[]{:S(2)}, u32[]{:S(2)}) %collective-permute-start.4) | collective-permute-done | bytes 98336 | tf_op jit(solution)/shard_map/ppermute | solution.py:184
  26.9 3.3 %shard_map.121 = (bf16[144,128]{1,0:T(8,128)(2,1)S(1)}, bf16[144,128]{1,0:T(8,128)(2,1)S(1)}, bf16[144,128]{1,0:T(8,128)(2,1)S(1)}, bf16[144,128]{1,0:T(8,128)(2...) custom-call(s32[1]{0:T(128)} %bitcast.index_ref, ...), custom_call_target="tpu_custom_call" | custom-call | flops 1000000000 | bytes 1311236 | tf_op jit(solution)/shard_map/pallas_call | solution.py:195
  30.2 4.0 %collective-permute-start.10 = (bf16[144,128]{1,0:T(8,128)(2,1)S(1)}, bf16[144,128]{1,0:T(8,128)(2,1)S(1)}, u32[]{:S(2)}, u32[]{:S(2)}) collective-permute-start(bf16[144,128]{1,0:T(8,128)(2,1)S(1)} %get-tuple-element.58), channel_id=1, source_target_pairs={{0,6},{1,7},{2,4},{3,5},{4,2},{5,3},{6,0},{7,1},{8,14},{9,15},{10,... | collective-permute-start | bytes 110600 | tf_op jit(solution)/shard_map/ppermute | solution.py:184
  35.4 2.6 %collective-permute-start.12 = (bf16[144,128]{1,0:T(8,128)(2,1)S(1)}, bf16[144,128]{1,0:T(8,128)(2,1)S(1)}, u32[]{:S(2)}, u32[]{:S(2)}) collective-permute-start(bf16[144,128]{1,0:T(8,128)(2,1)S(1)} %get-tuple-element.60), channel_id=1, source_target_pairs={{0,10},{1,11},{2,8},{3,9},{4,14},{5,15},{6,12},{7,13},{8,2},{9,3},... | collective-permute-start | bytes 110600 | tf_op jit(solution)/shard_map/ppermute | solution.py:184
  38.0 2.6 %collective-permute-start.13 = (bf16[144,128]{1,0:T(8,128)(2,1)S(1)}, bf16[144,128]{1,0:T(8,128)(2,1)S(1)}, u32[]{:S(2)}, u32[]{:S(2)}) collective-permute-start(bf16[144,128]{1,0:T(8,128)(2,1)S(1)} %get-tuple-element.61), channel_id=1, source_target_pairs={{0,12},{1,13},{2,14},{3,15},{4,8},{5,9},{6,10},{7,11},{8,4},{9,5},... | collective-permute-start | bytes 110600 | tf_op jit(solution)/shard_map/ppermute | solution.py:184
  40.7 2.3 %collective-permute-start.14 = (bf16[144,128]{1,0:T(8,128)(2,1)S(1)}, bf16[144,128]{1,0:T(8,128)(2,1)S(1)}, u32[]{:S(2)}, u32[]{:S(2)}) collective-permute-start(bf16[144,128]{1,0:T(8,128)(2,1)S(1)} %get-tuple-element.62), channel_id=1, source_target_pairs={{0,14},{1,15},{2,12},{3,13},{4,10},{5,11},{6,8},{7,9},{8,6},{9,7},... | collective-permute-start | bytes 110600 | tf_op jit(solution)/shard_map/ppermute | solution.py:184
  44.6 4.2 %shard_map.118 = (bf16[2048,256]{1,0:T(8,128)(2,1)S(1)}, bf16[2048,512]{1,0:T(8,128)(2,1)S(1)}, bf16[2048,256]{1,0:T(8,128)(2,1)S(1)}, bf16[512,2048]{1,0:T(8,12...) custom-call(bf16[2048,256]{1,0:T(8,128)(2,1)} %refs_0_.1, bf16[2048,512]{1,0:T(8,128)(2,1)} %bitcast.16, ...), custom_call_target="tpu_custom_call" | custom-call | bytes 11010048 | tf_op jit(solution)/shard_map/pallas_call | solution.py:195
  49.8 2.6 %collective-permute-start.38 = (bf16[64,2048]{1,0:T(8,128)(2,1)S(1)}, bf16[64,2048]{1,0:T(8,128)(2,1)S(1)}, u32[]{:S(2)}, u32[]{:S(2)}) collective-permute-start(bf16[64,2048]{1,0:T(8,128)(2,1)S(1)} %get-tuple-element.74), channel_id=1, source_target_pairs={{0,8},{1,9},{2,10},{3,11},{4,12},{5,13},{6,14},{7,15},{8,0},{9,1},... | collective-permute-start | bytes 786440 | tf_op jit(solution)/shard_map/ppermute | solution.py:184
  53.4 15.7 %collective-permute-done.38.refs_0_ = bf16[64,2048]{1,0:T(8,128)(2,1)S(1)} collective-permute-done((bf16[64,2048]{1,0:T(8,128)(2,1)S(1)}, bf16[64,2048]{1,0:T(8,128)(2,1)S(1)}, u32[]{:S(2)}, u32[]{:S(2)}) %collective-permute-start.38) | collective-permute-done | bytes 262176 | tf_op jit(solution)/shard_map/ppermute | solution.py:184
  69.1 5.8 %collective-permute-start.33 = (bf16[64,2048]{1,0:T(8,128)(2,1)S(1)}, bf16[64,2048]{1,0:T(8,128)(2,1)S(1)}, u32[]{:S(2)}, u32[]{:S(2)}) collective-permute-start(bf16[64,2048]{1,0:T(8,128)(2,1)S(1)} %get-tuple-element.71), channel_id=1, source_target_pairs={{0,8},{1,9},{2,10},{3,11},{4,12},{5,13},{6,14},{7,15},{8,0},{9,1},... | collective-permute-start | bytes 786440 | tf_op jit(solution)/shard_map/ppermute | solution.py:184
  74.8 11.2 %collective-permute-done.33.refs_0_ = bf16[64,2048]{1,0:T(8,128)(2,1)S(1)} collective-permute-done((bf16[64,2048]{1,0:T(8,128)(2,1)S(1)}, bf16[64,2048]{1,0:T(8,128)(2,1)S(1)}, u32[]{:S(2)}, u32[]{:S(2)}) %collective-permute-start.33) | collective-permute-done | bytes 262176 | tf_op jit(solution)/shard_map/ppermute | solution.py:184
  86.0 2.4 %collective-permute-start.25 = (bf16[64,2048]{1,0:T(8,128)(2,1)S(1)}, bf16[64,2048]{1,0:T(8,128)(2,1)S(1)}, u32[]{:S(2)}, u32[]{:S(2)}) collective-permute-start(bf16[64,2048]{1,0:T(8,128)(2,1)S(1)} %get-tuple-element.71), channel_id=1, source_target_pairs={{0,12},{1,13},{2,14},{3,15},{4,8},{5,9},{6,10},{7,11},{8,4},{9,5},... | collective-permute-start | bytes 786440 | tf_op jit(solution)/shard_map/ppermute | solution.py:184
  88.4 5.8 %collective-permute-done.25.refs_0_ = bf16[64,2048]{1,0:T(8,128)(2,1)S(1)} collective-permute-done((bf16[64,2048]{1,0:T(8,128)(2,1)S(1)}, bf16[64,2048]{1,0:T(8,128)(2,1)S(1)}, u32[]{:S(2)}, u32[]{:S(2)}) %collective-permute-start.25) | collective-permute-done | bytes 262176 | tf_op jit(solution)/shard_map/ppermute | solution.py:184
  97.4 16.4 %collective-permute-done.39.refs_1_ = bf16[64,2048]{1,0:T(8,128)(2,1)S(1)} collective-permute-done((bf16[64,2048]{1,0:T(8,128)(2,1)S(1)}, bf16[64,2048]{1,0:T(8,128)(2,1)S(1)}, u32[]{:S(2)}, u32[]{:S(2)}) %collective-permute-start.39) | collective-permute-done | bytes 262176 | tf_op jit(solution)/shard_map/ppermute | solution.py:184
  113.8 4.4 %collective-permute-start.20 = (bf16[128,2048]{1,0:T(8,128)(2,1)S(1)}, bf16[128,2048]{1,0:T(8,128)(2,1)S(1)}, u32[]{:S(2)}, u32[]{:S(2)}) collective-permute-start(bf16[128,2048]{1,0:T(8,128)(2,1)S(1)} %get-tuple-element.68.refs_0_), channel_id=1, source_target_pairs={{0,4},{1,5},{2,6},{3,7},{4,0},{5,1},{6,2},{7,3},{8,12},{9,13},{10,... | collective-permute-start | bytes 1572872 | tf_op jit(solution)/shard_map/ppermute | solution.py:184
  120.3 2.6 %shard_map.129 = (bf16[64,2048]{1,0:T(8,128)(2,1)S(1)}, bf16[64,2048]{1,0:T(8,128)(2,1)S(1)}) custom-call(s32[1]{0:T(128)} %bitcast.index_ref, bf16[2,2048]{1,0:T(2,128)(2,1)S(1)} %bitcast.6, bf16[2048,256]{1,0:T(8,128)(2,1)S(1)} %get-tuple-element.64.up_a, bf16[2048,256]{1,0:T(8,128)(2,1)S(1)} %collective-permute-done.15.up_b, ...), custom_call_target="tpu_custom_call" | custom-call | flops 1610612736 | bytes 13189124 | tf_op jit(solution)/shard_map/pallas_call | solution.py:195
  124.9 2.6 %shard_map.127 = (bf16[64,2048]{1,0:T(8,128)(2,1)S(1)}, bf16[64,2048]{1,0:T(8,128)(2,1)S(1)}) custom-call(s32[1]{0:T(128)} %bitcast.index_ref, bf16[2,2048]{1,0:T(2,128)(2,1)S(1)} %bitcast.7, bf16[2048,256]{1,0:T(8,128)(2,1)S(1)} %get-tuple-element.64.up_a, bf16[2048,256]{1,0:T(8,128)(2,1)S(1)} %collective-permute-done.15.up_b, ...), custom_call_target="tpu_custom_call" | custom-call | flops 1610612736 | bytes 13189124 | tf_op jit(solution)/shard_map/pallas_call | solution.py:195
  129.4 2.8 %shard_map.128 = (bf16[64,2048]{1,0:T(8,128)(2,1)S(1)}, bf16[64,2048]{1,0:T(8,128)(2,1)S(1)}) custom-call(s32[1]{0:T(128)} %bitcast.index_ref, bf16[2,2048]{1,0:T(2,128)(2,1)S(1)} %bitcast.8, bf16[2048,256]{1,0:T(8,128)(2,1)S(1)} %get-tuple-element.64.up_a, bf16[2048,256]{1,0:T(8,128)(2,1)S(1)} %collective-permute-done.15.up_b, ...), custom_call_target="tpu_custom_call" | custom-call | flops 1610612736 | bytes 13189124 | tf_op jit(solution)/shard_map/pallas_call | solution.py:195
  135.0 2.6 %shard_map.126 = (bf16[64,2048]{1,0:T(8,128)(2,1)S(1)}, bf16[64,2048]{1,0:T(8,128)(2,1)S(1)}) custom-call(s32[1]{0:T(128)} %bitcast.index_ref, bf16[2,2048]{1,0:T(2,128)(2,1)S(1)} %bitcast.9, bf16[2048,256]{1,0:T(8,128)(2,1)S(1)} %get-tuple-element.64.up_a, bf16[2048,256]{1,0:T(8,128)(2,1)S(1)} %collective-permute-done.15.up_b, ...), custom_call_target="tpu_custom_call" | custom-call | flops 1610612736 | bytes 13189124 | tf_op jit(solution)/shard_map/pallas_call | solution.py:195
  138.5 2.6 %shard_map.125 = bf16[128,2048]{1,0:T(8,128)(2,1)S(1)} custom-call(s32[1]{0:T(128)} %bitcast.index_ref, bf16[2,2048]{1,0:T(2,128)(2,1)S(1)} %bitcast.10, bf16[2048,256]{1,0:T(8,128)(2,1)S(1)} %get-tuple-element.64.up_a, bf16[2048,256]{1,0:T(8,128)(2,1)S(1)} %collective-permute-done.15.up_b, bf16[2048,512]{1,0:T(8,128)(2,1)S(1)} %get-tuple-element.65.in_a, ...), custom_call_target="tpu_custom_call" | custom-call | flops 1610612736 | bytes 13152260 | tf_op jit(solution)/shard_map/pallas_call | solution.py:195
  142.9 2.6 %shard_map.124 = bf16[128,2048]{1,0:T(8,128)(2,1)S(1)} custom-call(s32[1]{0:T(128)} %bitcast.index_ref, bf16[2,2048]{1,0:T(2,128)(2,1)S(1)} %bitcast.11, bf16[2048,256]{1,0:T(8,128)(2,1)S(1)} %get-tuple-element.64.up_a, bf16[2048,256]{1,0:T(8,128)(2,1)S(1)} %collective-permute-done.15.up_b, bf16[2048,512]{1,0:T(8,128)(2,1)S(1)} %get-tuple-element.65.in_a, ...), custom_call_target="tpu_custom_call" | custom-call | flops 1610612736 | bytes 13152260 | tf_op jit(solution)/shard_map/pallas_call | solution.py:195
  145.5 3.9 %shard_map.123 = (bf16[128,2048]{1,0:T(8,128)(2,1)S(1)}, bf16[128,2048]{1,0:T(8,128)(2,1)S(1)}) custom-call(s32[1]{0:T(128)} %bitcast.index_ref, bf16[2,2048]{1,0:T(2,128)(2,1)S(1)} %bitcast.12, bf16[2048,256]{1,0:T(8,128)(2,1)S(1)} %get-tuple-element.64.up_a, bf16[2048,256]{1,0:T(8,128)(2,1)S(1)} %collective-permute-done.15.up_b, ...), custom_call_target="tpu_custom_call" | custom-call | flops 3221225472 | bytes 13713412 | tf_op jit(solution)/shard_map/pallas_call | solution.py:195
  150.3 6.8 %collective-permute-start.41 = (bf16[64,2048]{1,0:T(8,128)(2,1)S(1)}, bf16[64,2048]{1,0:T(8,128)(2,1)S(1)}, u32[]{:S(2)}, u32[]{:S(2)}) collective-permute-start(bf16[64,2048]{1,0:T(8,128)(2,1)S(1)} %add_convert_fusion.3), channel_id=1, source_target_pairs={{0,4},{1,5},{2,6},{3,7},{12,8},{13,9},{14,10},{15,11},{16,20},{17,... | collective-permute-start | bytes 786440 | tf_op jit(solution)/shard_map/ppermute | solution.py:184
  157.9 9.4 %collective-permute-done.41 = bf16[64,2048]{1,0:T(8,128)(2,1)S(1)} collective-permute-done((bf16[64,2048]{1,0:T(8,128)(2,1)S(1)}, bf16[64,2048]{1,0:T(8,128)(2,1)S(1)}, u32[]{:S(2)}, u32[]{:S(2)}) %collective-permute-start.41) | collective-permute-done | bytes 262176 | tf_op jit(solution)/shard_map/ppermute | solution.py:184
  167.4 4.4 %collective-permute-start.36 = (bf16[64,2048]{1,0:T(8,128)(2,1)S(1)}, bf16[64,2048]{1,0:T(8,128)(2,1)S(1)}, u32[]{:S(2)}, u32[]{:S(2)}) collective-permute-start(bf16[64,2048]{1,0:T(8,128)(2,1)S(1)} %add_convert_fusion.4), channel_id=1, source_target_pairs={{0,4},{1,5},{2,6},{3,7},{12,8},{13,9},{14,10},{15,11},{16,20},{17,... | collective-permute-start | bytes 786440 | tf_op jit(solution)/shard_map/ppermute | solution.py:184
  172.7 2.1 %collective-permute-start.42 = (bf16[64,2048]{1,0:T(8,128)(2,1)S(1)}, bf16[64,2048]{1,0:T(8,128)(2,1)S(1)}, u32[]{:S(2)}, u32[]{:S(2)}) collective-permute-start(bf16[64,2048]{1,0:T(8,128)(2,1)S(1)} %add_convert_fusion.1), channel_id=1, source_target_pairs={{0,8},{1,9},{2,10},{3,11},{4,12},{5,13},{6,14},{7,15},{8,0},{9,1},... | collective-permute-start | bytes 786440 | tf_op jit(solution)/shard_map/ppermute | solution.py:184
  174.8 3.4 %collective-permute-done.36 = bf16[64,2048]{1,0:T(8,128)(2,1)S(1)} collective-permute-done((bf16[64,2048]{1,0:T(8,128)(2,1)S(1)}, bf16[64,2048]{1,0:T(8,128)(2,1)S(1)}, u32[]{:S(2)}, u32[]{:S(2)}) %collective-permute-start.36) | collective-permute-done | bytes 262176 | tf_op jit(solution)/shard_map/ppermute | solution.py:184
  180.9 13.5 %collective-permute-done.42.refs_6_ = bf16[64,2048]{1,0:T(8,128)(2,1)S(1)} collective-permute-done((bf16[64,2048]{1,0:T(8,128)(2,1)S(1)}, bf16[64,2048]{1,0:T(8,128)(2,1)S(1)}, u32[]{:S(2)}, u32[]{:S(2)}) %collective-permute-start.42) | collective-permute-done | bytes 262176 | tf_op jit(solution)/shard_map/ppermute | solution.py:184
  194.3 2.8 %collective-permute-done.37.refs_5_ = bf16[64,2048]{1,0:T(8,128)(2,1)S(1)} collective-permute-done((bf16[64,2048]{1,0:T(8,128)(2,1)S(1)}, bf16[64,2048]{1,0:T(8,128)(2,1)S(1)}, u32[]{:S(2)}, u32[]{:S(2)}) %collective-permute-start.37) | collective-permute-done | bytes 262176 | tf_op jit(solution)/shard_map/ppermute | solution.py:184
  (82 shorter events, 32.8 us)
Async XLA Ops:
  1.3 8.9 %collective-permute-start = (bf16[128,384]{1,0:T(8,128)(2,1)S(1)}, bf16[128,384]{1,0:T(8,128)(2,1)S(1)}, u32[]{:S(2)}, u32[]{:S(2)}) collective-permute-start(bf16[128,384]{1,0:T(8,128)(2,1)S(1)} %get-tuple-element.46), channel_id=1, source_target_pairs={{0,2},{1,3},{2,0},{3,1},{4,6},{5,7},{6,4},{7,5},{8,10},{9,11},{10,... | collective-permute-start | bytes 294920 | tf_op jit(solution)/shard_map/ppermute | solution.py:184
  4.4 9.5 %collective-permute-start.1 = (bf16[128,384]{1,0:T(8,128)(2,1)S(1)}, bf16[128,384]{1,0:T(8,128)(2,1)S(1)}, u32[]{:S(2)}, u32[]{:S(2)}) collective-permute-start(bf16[128,384]{1,0:T(8,128)(2,1)S(1)} %get-tuple-element.47), channel_id=1, source_target_pairs={{0,4},{1,5},{2,6},{3,7},{4,0},{5,1},{6,2},{7,3},{8,12},{9,13},{10,... | collective-permute-start | bytes 294920 | tf_op jit(solution)/shard_map/ppermute | solution.py:184
  8.9 15.2 %collective-permute-start.4 = (bf16[128,384]{1,0:T(8,128)(2,1)S(1)}, bf16[128,384]{1,0:T(8,128)(2,1)S(1)}, u32[]{:S(2)}, u32[]{:S(2)}) collective-permute-start(bf16[128,384]{1,0:T(8,128)(2,1)S(1)} %get-tuple-element.50), channel_id=1, source_target_pairs={{0,10},{1,11},{2,8},{3,9},{4,14},{5,15},{6,12},{7,13},{8,2},{9,3},... | collective-permute-start | bytes 294920 | tf_op jit(solution)/shard_map/ppermute | solution.py:184
  10.2 13.9 %collective-permute-start.5 = (bf16[128,384]{1,0:T(8,128)(2,1)S(1)}, bf16[128,384]{1,0:T(8,128)(2,1)S(1)}, u32[]{:S(2)}, u32[]{:S(2)}) collective-permute-start(bf16[128,384]{1,0:T(8,128)(2,1)S(1)} %get-tuple-element.51), channel_id=1, source_target_pairs={{0,12},{1,13},{2,14},{3,15},{4,8},{5,9},{6,10},{7,11},{8,4},{9,5},... | collective-permute-start | bytes 294920 | tf_op jit(solution)/shard_map/ppermute | solution.py:184
  13.8 10.3 %collective-permute-start.6 = (bf16[128,384]{1,0:T(8,128)(2,1)S(1)}, bf16[128,384]{1,0:T(8,128)(2,1)S(1)}, u32[]{:S(2)}, u32[]{:S(2)}) collective-permute-start(bf16[128,384]{1,0:T(8,128)(2,1)S(1)} %get-tuple-element.52), channel_id=1, source_target_pairs={{0,14},{1,15},{2,12},{3,13},{4,10},{5,11},{6,8},{7,9},{8,6},{9,7},... | collective-permute-start | bytes 294920 | tf_op jit(solution)/shard_map/ppermute | solution.py:184
  24.3 95.9 %collective-permute-start.16 = (bf16[2048,512]{1,0:T(8,128)(2,1)}, bf16[2048,512]{1,0:T(8,128)(2,1)S(1)}, u32[]{:S(2)}, u32[]{:S(2)}) collective-permute-start(bf16[2048,512]{1,0:T(8,128)(2,1)} %bitcast.15), channel_id=1, source_target_pairs={{0,1},{1,0},{2,3},{3,2},{4,5},{5,4},{6,7},{7,6},{8,9},{9,8},{10,11... | collective-permute-start | bytes 6291464 | tf_op jit(solution)/shard_map/ppermute | solution.py:184
  24.8 95.5 %collective-permute-start.18 = (bf16[512,2048]{1,0:T(8,128)(2,1)}, bf16[512,2048]{1,0:T(8,128)(2,1)S(1)}, u32[]{:S(2)}, u32[]{:S(2)}) collective-permute-start(bf16[512,2048]{1,0:T(8,128)(2,1)} %bitcast.17), channel_id=1, source_target_pairs={{0,1},{1,0},{2,3},{3,2},{4,5},{5,4},{6,7},{7,6},{8,9},{9,8},{10,11... | collective-permute-start | bytes 6291464 | tf_op jit(solution)/shard_map/ppermute | solution.py:184
  49.8 19.3 %collective-permute-start.38 = (bf16[64,2048]{1,0:T(8,128)(2,1)S(1)}, bf16[64,2048]{1,0:T(8,128)(2,1)S(1)}, u32[]{:S(2)}, u32[]{:S(2)}) collective-permute-start(bf16[64,2048]{1,0:T(8,128)(2,1)S(1)} %get-tuple-element.74), channel_id=1, source_target_pairs={{0,8},{1,9},{2,10},{3,11},{4,12},{5,13},{6,14},{7,15},{8,0},{9,1},... | collective-permute-start | bytes 786440 | tf_op jit(solution)/shard_map/ppermute | solution.py:184
  52.4 16.6 %collective-permute-start.29 = (bf16[64,2048]{1,0:T(8,128)(2,1)S(1)}, bf16[64,2048]{1,0:T(8,128)(2,1)S(1)}, u32[]{:S(2)}, u32[]{:S(2)}) collective-permute-start(bf16[64,2048]{1,0:T(8,128)(2,1)S(1)} %get-tuple-element.74), channel_id=1, source_target_pairs={{0,12},{1,13},{2,14},{3,15},{4,8},{5,9},{6,10},{7,11},{8,4},{9,5},... | collective-permute-start | bytes 786440 | tf_op jit(solution)/shard_map/ppermute | solution.py:184
  53.4 42.0 %collective-permute-start.15 = (bf16[2048,256]{1,0:T(8,128)(2,1)S(1)}, bf16[2048,256]{1,0:T(8,128)(2,1)S(1)}, u32[]{:S(2)}, u32[]{:S(2)}) collective-permute-start(bf16[2048,256]{1,0:T(8,128)(2,1)S(1)} %copy-done.3), channel_id=1, source_target_pairs={{0,1},{1,0},{2,3},{3,2},{4,5},{5,4},{6,7},{7,6},{8,9},{9,8},{10,11... | collective-permute-start | bytes 3145736 | tf_op jit(solution)/shard_map/ppermute | solution.py:184
  69.1 27.2 %collective-permute-start.17 = (bf16[2048,256]{1,0:T(8,128)(2,1)S(1)}, bf16[2048,256]{1,0:T(8,128)(2,1)S(1)}, u32[]{:S(2)}, u32[]{:S(2)}) collective-permute-start(bf16[2048,256]{1,0:T(8,128)(2,1)S(1)} %copy-done.4), channel_id=1, source_target_pairs={{0,1},{1,0},{2,3},{3,2},{4,5},{5,4},{6,7},{7,6},{8,9},{9,8},{10,11... | collective-permute-start | bytes 3145736 | tf_op jit(solution)/shard_map/ppermute | solution.py:184
  69.1 17.0 %collective-permute-start.33 = (bf16[64,2048]{1,0:T(8,128)(2,1)S(1)}, bf16[64,2048]{1,0:T(8,128)(2,1)S(1)}, u32[]{:S(2)}, u32[]{:S(2)}) collective-permute-start(bf16[64,2048]{1,0:T(8,128)(2,1)S(1)} %get-tuple-element.71), channel_id=1, source_target_pairs={{0,8},{1,9},{2,10},{3,11},{4,12},{5,13},{6,14},{7,15},{8,0},{9,1},... | collective-permute-start | bytes 786440 | tf_op jit(solution)/shard_map/ppermute | solution.py:184
  94.2 24.0 %collective-permute-start.19 = (bf16[128,2048]{1,0:T(8,128)(2,1)S(1)}, bf16[128,2048]{1,0:T(8,128)(2,1)S(1)}, u32[]{:S(2)}, u32[]{:S(2)}) collective-permute-start(bf16[128,2048]{1,0:T(8,128)(2,1)S(1)} %get-tuple-element.68.refs_0_), channel_id=1, source_target_pairs={{0,2},{1,3},{2,0},{3,1},{4,6},{5,7},{6,4},{7,5},{8,10},{9,11},{10,... | collective-permute-start | bytes 1572872 | tf_op jit(solution)/shard_map/ppermute | solution.py:184
  95.4 18.5 %collective-permute-start.39 = (bf16[64,2048]{1,0:T(8,128)(2,1)S(1)}, bf16[64,2048]{1,0:T(8,128)(2,1)S(1)}, u32[]{:S(2)}, u32[]{:S(2)}) collective-permute-start(bf16[64,2048]{1,0:T(8,128)(2,1)S(1)} %collective-permute-done.38.refs_0_), channel_id=1, source_target_pairs={{0,2},{1,3},{2,0},{3,1},{4,6},{5,7},{6,4},{7,5},{8,10},{9,11},{10,... | collective-permute-start | bytes 786440 | tf_op jit(solution)/shard_map/ppermute | solution.py:184
  96.2 26.7 %collective-permute-start.30 = (bf16[64,2048]{1,0:T(8,128)(2,1)S(1)}, bf16[64,2048]{1,0:T(8,128)(2,1)S(1)}, u32[]{:S(2)}, u32[]{:S(2)}) collective-permute-start(bf16[64,2048]{1,0:T(8,128)(2,1)S(1)} %collective-permute-done.29.refs_0_), channel_id=1, source_target_pairs={{0,2},{1,3},{2,0},{3,1},{4,6},{5,7},{6,4},{7,5},{8,10},{9,11},{10,... | collective-permute-start | bytes 786440 | tf_op jit(solution)/shard_map/ppermute | solution.py:184
  113.8 27.2 %collective-permute-start.20 = (bf16[128,2048]{1,0:T(8,128)(2,1)S(1)}, bf16[128,2048]{1,0:T(8,128)(2,1)S(1)}, u32[]{:S(2)}, u32[]{:S(2)}) collective-permute-start(bf16[128,2048]{1,0:T(8,128)(2,1)S(1)} %get-tuple-element.68.refs_0_), channel_id=1, source_target_pairs={{0,4},{1,5},{2,6},{3,7},{4,0},{5,1},{6,2},{7,3},{8,12},{9,13},{10,... | collective-permute-start | bytes 1572872 | tf_op jit(solution)/shard_map/ppermute | solution.py:184
  118.2 9.3 %collective-permute-start.34 = (bf16[64,2048]{1,0:T(8,128)(2,1)S(1)}, bf16[64,2048]{1,0:T(8,128)(2,1)S(1)}, u32[]{:S(2)}, u32[]{:S(2)}) collective-permute-start(bf16[64,2048]{1,0:T(8,128)(2,1)S(1)} %collective-permute-done.33.refs_0_), channel_id=1, source_target_pairs={{0,2},{1,3},{2,0},{3,1},{4,6},{5,7},{6,4},{7,5},{8,10},{9,11},{10,... | collective-permute-start | bytes 786440 | tf_op jit(solution)/shard_map/ppermute | solution.py:184
  120.2 12.8 %collective-permute-start.26 = (bf16[64,2048]{1,0:T(8,128)(2,1)S(1)}, bf16[64,2048]{1,0:T(8,128)(2,1)S(1)}, u32[]{:S(2)}, u32[]{:S(2)}) collective-permute-start(bf16[64,2048]{1,0:T(8,128)(2,1)S(1)} %collective-permute-done.25.refs_0_), channel_id=1, source_target_pairs={{0,2},{1,3},{2,0},{3,1},{4,6},{5,7},{6,4},{7,5},{8,10},{9,11},{10,... | collective-permute-start | bytes 786440 | tf_op jit(solution)/shard_map/ppermute | solution.py:184
  120.3 17.3 %collective-permute-start.22 = (bf16[128,2048]{1,0:T(8,128)(2,1)S(1)}, bf16[128,2048]{1,0:T(8,128)(2,1)S(1)}, u32[]{:S(2)}, u32[]{:S(2)}) collective-permute-start(bf16[128,2048]{1,0:T(8,128)(2,1)S(1)} %collective-permute-done.19.refs_1_), channel_id=1, source_target_pairs={{0,4},{1,5},{2,6},{3,7},{4,0},{5,1},{6,2},{7,3},{8,12},{9,13},{10,... | collective-permute-start | bytes 1572872 | tf_op jit(solution)/shard_map/ppermute | solution.py:184
  122.9 34.3 %collective-permute-start.40 = (bf16[64,2048]{1,0:T(8,128)(2,1)S(1)}, bf16[64,2048]{1,0:T(8,128)(2,1)S(1)}, u32[]{:S(2)}, u32[]{:S(2)}) collective-permute-start(bf16[64,2048]{1,0:T(8,128)(2,1)S(1)} %get-tuple-element.80), channel_id=1, source_target_pairs={{0,2},{1,3},{2,0},{3,1},{4,6},{5,7},{6,4},{7,5},{8,10},{9,11},{10,... | collective-permute-start | bytes 786440 | tf_op jit(solution)/shard_map/ppermute | solution.py:184
  127.5 21.9 %collective-permute-start.31 = (bf16[64,2048]{1,0:T(8,128)(2,1)S(1)}, bf16[64,2048]{1,0:T(8,128)(2,1)S(1)}, u32[]{:S(2)}, u32[]{:S(2)}) collective-permute-start(bf16[64,2048]{1,0:T(8,128)(2,1)S(1)} %get-tuple-element.76), channel_id=1, source_target_pairs={{0,2},{1,3},{2,0},{3,1},{4,6},{5,7},{6,4},{7,5},{8,10},{9,11},{10,... | collective-permute-start | bytes 786440 | tf_op jit(solution)/shard_map/ppermute | solution.py:184
  133.0 39.7 %collective-permute-start.35 = (bf16[64,2048]{1,0:T(8,128)(2,1)S(1)}, bf16[64,2048]{1,0:T(8,128)(2,1)S(1)}, u32[]{:S(2)}, u32[]{:S(2)}) collective-permute-start(bf16[64,2048]{1,0:T(8,128)(2,1)S(1)} %get-tuple-element.78), channel_id=1, source_target_pairs={{0,2},{1,3},{2,0},{3,1},{4,6},{5,7},{6,4},{7,5},{8,10},{9,11},{10,... | collective-permute-start | bytes 786440 | tf_op jit(solution)/shard_map/ppermute | solution.py:184
  137.6 12.7 %collective-permute-start.27 = (bf16[64,2048]{1,0:T(8,128)(2,1)S(1)}, bf16[64,2048]{1,0:T(8,128)(2,1)S(1)}, u32[]{:S(2)}, u32[]{:S(2)}) collective-permute-start(bf16[64,2048]{1,0:T(8,128)(2,1)S(1)} %get-tuple-element.73), channel_id=1, source_target_pairs={{0,2},{1,3},{2,0},{3,1},{4,6},{5,7},{6,4},{7,5},{8,10},{9,11},{10,... | collective-permute-start | bytes 786440 | tf_op jit(solution)/shard_map/ppermute | solution.py:184
  141.1 30.8 %collective-permute-start.23 = (bf16[128,2048]{1,0:T(8,128)(2,1)S(1)}, bf16[128,2048]{1,0:T(8,128)(2,1)S(1)}, u32[]{:S(2)}, u32[]{:S(2)}) collective-permute-start(bf16[128,2048]{1,0:T(8,128)(2,1)S(1)} %shard_map.125), channel_id=1, source_target_pairs={{0,4},{1,5},{2,6},{3,7},{4,0},{5,1},{6,2},{7,3},{8,12},{9,13},{10,... | collective-permute-start | bytes 1572872 | tf_op jit(solution)/shard_map/ppermute | solution.py:184
  149.4 31.4 %collective-permute-start.21 = (bf16[128,2048]{1,0:T(8,128)(2,1)S(1)}, bf16[128,2048]{1,0:T(8,128)(2,1)S(1)}, u32[]{:S(2)}, u32[]{:S(2)}) collective-permute-start(bf16[128,2048]{1,0:T(8,128)(2,1)S(1)} %shard_map.124), channel_id=1, source_target_pairs={{0,4},{1,5},{2,6},{3,7},{4,0},{5,1},{6,2},{7,3},{8,12},{9,13},{10,... | collective-permute-start | bytes 1572872 | tf_op jit(solution)/shard_map/ppermute | solution.py:184
  150.3 17.0 %collective-permute-start.41 = (bf16[64,2048]{1,0:T(8,128)(2,1)S(1)}, bf16[64,2048]{1,0:T(8,128)(2,1)S(1)}, u32[]{:S(2)}, u32[]{:S(2)}) collective-permute-start(bf16[64,2048]{1,0:T(8,128)(2,1)S(1)} %add_convert_fusion.3), channel_id=1, source_target_pairs={{0,4},{1,5},{2,6},{3,7},{12,8},{13,9},{14,10},{15,11},{16,20},{17,... | collective-permute-start | bytes 786440 | tf_op jit(solution)/shard_map/ppermute | solution.py:184
  157.2 22.9 %collective-permute-start.32 = (bf16[64,2048]{1,0:T(8,128)(2,1)S(1)}, bf16[64,2048]{1,0:T(8,128)(2,1)S(1)}, u32[]{:S(2)}, u32[]{:S(2)}) collective-permute-start(bf16[64,2048]{1,0:T(8,128)(2,1)S(1)} %add_convert_fusion.3), channel_id=1, source_target_pairs={{4,8},{5,9},{6,10},{7,11},{8,4},{9,5},{10,6},{11,7},{20,24},{21,25... | collective-permute-start | bytes 786440 | tf_op jit(solution)/shard_map/ppermute | solution.py:184
  167.4 10.9 %collective-permute-start.36 = (bf16[64,2048]{1,0:T(8,128)(2,1)S(1)}, bf16[64,2048]{1,0:T(8,128)(2,1)S(1)}, u32[]{:S(2)}, u32[]{:S(2)}) collective-permute-start(bf16[64,2048]{1,0:T(8,128)(2,1)S(1)} %add_convert_fusion.4), channel_id=1, source_target_pairs={{0,4},{1,5},{2,6},{3,7},{12,8},{13,9},{14,10},{15,11},{16,20},{17,... | collective-permute-start | bytes 786440 | tf_op jit(solution)/shard_map/ppermute | solution.py:184
  171.9 9.0 %collective-permute-start.28 = (bf16[64,2048]{1,0:T(8,128)(2,1)S(1)}, bf16[64,2048]{1,0:T(8,128)(2,1)S(1)}, u32[]{:S(2)}, u32[]{:S(2)}) collective-permute-start(bf16[64,2048]{1,0:T(8,128)(2,1)S(1)} %add_convert_fusion.4), channel_id=1, source_target_pairs={{4,8},{5,9},{6,10},{7,11},{8,4},{9,5},{10,6},{11,7},{20,24},{21,25... | collective-permute-start | bytes 786440 | tf_op jit(solution)/shard_map/ppermute | solution.py:184
  172.7 21.6 %collective-permute-start.42 = (bf16[64,2048]{1,0:T(8,128)(2,1)S(1)}, bf16[64,2048]{1,0:T(8,128)(2,1)S(1)}, u32[]{:S(2)}, u32[]{:S(2)}) collective-permute-start(bf16[64,2048]{1,0:T(8,128)(2,1)S(1)} %add_convert_fusion.1), channel_id=1, source_target_pairs={{0,8},{1,9},{2,10},{3,11},{4,12},{5,13},{6,14},{7,15},{8,0},{9,1},... | collective-permute-start | bytes 786440 | tf_op jit(solution)/shard_map/ppermute | solution.py:184
  178.2 18.9 %collective-permute-start.24 = (bf16[128,2048]{1,0:T(8,128)(2,1)S(1)}, bf16[128,2048]{1,0:T(8,128)(2,1)S(1)}, u32[]{:S(2)}, u32[]{:S(2)}) collective-permute-start(bf16[128,2048]{1,0:T(8,128)(2,1)S(1)} %add_convert_fusion), channel_id=1, source_target_pairs={{0,2},{1,3},{2,0},{3,1},{4,6},{5,7},{6,4},{7,5},{8,10},{9,11},{10,... | collective-permute-start | bytes 1572872 | tf_op jit(solution)/shard_map/ppermute | solution.py:184
  180.1 17.1 %collective-permute-start.37 = (bf16[64,2048]{1,0:T(8,128)(2,1)S(1)}, bf16[64,2048]{1,0:T(8,128)(2,1)S(1)}, u32[]{:S(2)}, u32[]{:S(2)}) collective-permute-start(bf16[64,2048]{1,0:T(8,128)(2,1)S(1)} %add_convert_fusion.2), channel_id=1, source_target_pairs={{0,8},{1,9},{2,10},{3,11},{4,12},{5,13},{6,14},{7,15},{8,0},{9,1},... | collective-permute-start | bytes 786440 | tf_op jit(solution)/shard_map/ppermute | solution.py:184
  (16 other events, 174.5 us)

commit v3 on v2

--- a/solution.py
+++ b/solution.py
@@ -471,18 +471,18 @@
     arrived, passed = [], {}
     for offset in (12, 8):
         for half, rows_sent in zip("ab", halves):
+            name = f"{offset}{half}"
             first = swap(rows_sent, offset)
             second = swap(first, 2)
             start = 0 if half == "a" else rows // 2
             part, part_across = mix({offset: first, offset | 2: second}, start)
             returned = swap(part_across, 2)
-            if offset == 12:
-                summed = plus(part, returned)
+            summed = plus(part, returned, *passed.get(name, ()))
+            if name == "12b":
                 arrived.append(swap(summed, 12, inner))
-                passed[half] = swap(summed, 4, outer)
+                passed["8b"] = [swap(summed, 4, outer)]
             else:
-                summed = plus(part, returned, passed[half])
-                arrived.append(swap(summed, 8))
+                arrived.append(swap(summed, offset))
     part, part_across = mix({0: normed, 2: across})
     (part_beside,) = mix({4: beside})
     (part_both,) = mix({6: beside_across})

time: 199 us -> 184 us (0.925)
  waiting for transfers between devices: 91.5 us -> 61.3 us
  starting transfers between devices: 74.8 us -> 90.9 us
    ppermute x43 -> x42, waiting for transfers between devices: 91.5 us -> 61.3 us  [swap(): return lax.ppermute(array, 'ctx', pairs)]
    ppermute x43 -> x42, starting transfers between devices: 74.8 us -> 90.9 us  [swap(): return lax.ppermute(array, 'ctx', pairs)]
  transfers between devices with their start and end apart: 43 -> 42, of which waited for: 13 -> 14; matrix products, arithmetic and copies ran while one was open for 0% -> 0% of each run, Pallas kernels for 14% -> 15%
where the time goes in v3:
time: 184 us
  starting transfers between devices  90.9 us (49%)
  waiting for transfers between devices  61.3 us (33%)
  Pallas kernels  30.6 us (17%)
    ppermute x42, starting transfers between devices, swap(): return lax.ppermute(array, 'ctx', pairs)  90.9 us
    ppermute x42, waiting for transfers between devices, swap(): return lax.ppermute(array, 'ctx', pairs)  61.3 us
    pallas_call x13, Pallas kernels, call(): pl.pallas_call(kernel, out_shape=outs, in_specs=specs, out_specs=[VMEM] *...  30.6 us
  transfers between devices with their start and end apart: 42, of which 14 were waited for; matrix products, arithmetic and copies ran while one was open for 0% of the time, Pallas kernels for 15%

profile of v3, /device:TPU:0, one launch (start us, length us, event | category | flops | bytes accessed | tf_op | source)
XLA Modules:
  0.0 184.2 jit_solution(3201975678892699686)
XLA Ops:
  1.3 3.1 %collective-permute-start = (bf16[128,384]{1,0:T(8,128)(2,1)S(1)}, bf16[128,384]{1,0:T(8,128)(2,1)S(1)}, u32[]{:S(2)}, u32[]{:S(2)}) collective-permute-start(bf16[128,384]{1,0:T(8,128)(2,1)S(1)} %get-tuple-element.46), channel_id=1, source_target_pairs={{0,2},{1,3},{2,0},{3,1},{4,6},{5,7},{6,4},{7,5},{8,10},{9,11},{10,... | collective-permute-start | bytes 294920 | tf_op jit(solution)/shard_map/ppermute | solution.py:184
  6.0 3.0 %collective-permute-start.3 = (bf16[128,384]{1,0:T(8,128)(2,1)S(1)}, bf16[128,384]{1,0:T(8,128)(2,1)S(1)}, u32[]{:S(2)}, u32[]{:S(2)}) collective-permute-start(bf16[128,384]{1,0:T(8,128)(2,1)S(1)} %get-tuple-element.49), channel_id=1, source_target_pairs={{0,8},{1,9},{2,10},{3,11},{4,12},{5,13},{6,14},{7,15},{8,0},{9,1},... | collective-permute-start | bytes 294920 | tf_op jit(solution)/shard_map/ppermute | solution.py:184
  10.2 3.6 %collective-permute-start.5 = (bf16[128,384]{1,0:T(8,128)(2,1)S(1)}, bf16[128,384]{1,0:T(8,128)(2,1)S(1)}, u32[]{:S(2)}, u32[]{:S(2)}) collective-permute-start(bf16[128,384]{1,0:T(8,128)(2,1)S(1)} %get-tuple-element.51), channel_id=1, source_target_pairs={{0,12},{1,13},{2,14},{3,15},{4,8},{5,9},{6,10},{7,11},{8,4},{9,5},... | collective-permute-start | bytes 294920 | tf_op jit(solution)/shard_map/ppermute | solution.py:184
  13.9 10.3 %collective-permute-done.4.refs_5_ = bf16[128,384]{1,0:T(8,128)(2,1)S(1)} collective-permute-done((bf16[128,384]{1,0:T(8,128)(2,1)S(1)}, bf16[128,384]{1,0:T(8,128)(2,1)S(1)}, u32[]{:S(2)}, u32[]{:S(2)}) %collective-permute-start.4) | collective-permute-done | bytes 98336 | tf_op jit(solution)/shard_map/ppermute | solution.py:184
  26.9 3.3 %shard_map.121 = (bf16[144,128]{1,0:T(8,128)(2,1)S(1)}, bf16[144,128]{1,0:T(8,128)(2,1)S(1)}, bf16[144,128]{1,0:T(8,128)(2,1)S(1)}, bf16[144,128]{1,0:T(8,128)(2...) custom-call(s32[1]{0:T(128)} %bitcast.index_ref, ...), custom_call_target="tpu_custom_call" | custom-call | flops 1000000000 | bytes 1311236 | tf_op jit(solution)/shard_map/pallas_call | solution.py:195
  31.1 3.6 %collective-permute-start.9 = (bf16[144,128]{1,0:T(8,128)(2,1)S(1)}, bf16[144,128]{1,0:T(8,128)(2,1)S(1)}, u32[]{:S(2)}, u32[]{:S(2)}) collective-permute-start(bf16[144,128]{1,0:T(8,128)(2,1)S(1)} %get-tuple-element.57), channel_id=1, source_target_pairs={{0,4},{1,5},{2,6},{3,7},{4,0},{5,1},{6,2},{7,3},{8,12},{9,13},{10,... | collective-permute-start | bytes 110600 | tf_op jit(solution)/shard_map/ppermute | solution.py:184
  35.7 3.6 %collective-permute-start.11 = (bf16[144,128]{1,0:T(8,128)(2,1)S(1)}, bf16[144,128]{1,0:T(8,128)(2,1)S(1)}, u32[]{:S(2)}, u32[]{:S(2)}) collective-permute-start(bf16[144,128]{1,0:T(8,128)(2,1)S(1)} %get-tuple-element.59), channel_id=1, source_target_pairs={{0,8},{1,9},{2,10},{3,11},{4,12},{5,13},{6,14},{7,15},{8,0},{9,1},... | collective-permute-start | bytes 110600 | tf_op jit(solution)/shard_map/ppermute | solution.py:184
  42.3 2.5 %collective-permute-start.14 = (bf16[144,128]{1,0:T(8,128)(2,1)S(1)}, bf16[144,128]{1,0:T(8,128)(2,1)S(1)}, u32[]{:S(2)}, u32[]{:S(2)}) collective-permute-start(bf16[144,128]{1,0:T(8,128)(2,1)S(1)} %get-tuple-element.62), channel_id=1, source_target_pairs={{0,14},{1,15},{2,12},{3,13},{4,10},{5,11},{6,8},{7,9},{8,6},{9,7},... | collective-permute-start | bytes 110600 | tf_op jit(solution)/shard_map/ppermute | solution.py:184
  44.8 4.2 %shard_map.118 = (bf16[2048,256]{1,0:T(8,128)(2,1)S(1)}, bf16[2048,512]{1,0:T(8,128)(2,1)S(1)}, bf16[2048,256]{1,0:T(8,128)(2,1)S(1)}, bf16[512,2048]{1,0:T(8,12...) custom-call(bf16[2048,256]{1,0:T(8,128)(2,1)} %refs_0_.1, bf16[2048,512]{1,0:T(8,128)(2,1)} %bitcast.16, ...), custom_call_target="tpu_custom_call" | custom-call | bytes 11010048 | tf_op jit(solution)/shard_map/pallas_call | solution.py:195
  50.0 2.4 %collective-permute-start.25 = (bf16[64,2048]{1,0:T(8,128)(2,1)S(1)}, bf16[64,2048]{1,0:T(8,128)(2,1)S(1)}, u32[]{:S(2)}, u32[]{:S(2)}) collective-permute-start(bf16[64,2048]{1,0:T(8,128)(2,1)S(1)} %get-tuple-element.71), channel_id=1, source_target_pairs={{0,12},{1,13},{2,14},{3,15},{4,8},{5,9},{6,10},{7,11},{8,4},{9,5},... | collective-permute-start | bytes 786440 | tf_op jit(solution)/shard_map/ppermute | solution.py:184
  53.9 5.2 %collective-permute-done.25.refs_0_ = bf16[64,2048]{1,0:T(8,128)(2,1)S(1)} collective-permute-done((bf16[64,2048]{1,0:T(8,128)(2,1)S(1)}, bf16[64,2048]{1,0:T(8,128)(2,1)S(1)}, u32[]{:S(2)}, u32[]{:S(2)}) %collective-permute-start.25) | collective-permute-done | bytes 262176 | tf_op jit(solution)/shard_map/ppermute | solution.py:184
  59.1 14.2 %collective-permute-start.33 = (bf16[64,2048]{1,0:T(8,128)(2,1)S(1)}, bf16[64,2048]{1,0:T(8,128)(2,1)S(1)}, u32[]{:S(2)}, u32[]{:S(2)}) collective-permute-start(bf16[64,2048]{1,0:T(8,128)(2,1)S(1)} %get-tuple-element.71), channel_id=1, source_target_pairs={{0,8},{1,9},{2,10},{3,11},{4,12},{5,13},{6,14},{7,15},{8,0},{9,1},... | collective-permute-start | bytes 786440 | tf_op jit(solution)/shard_map/ppermute | solution.py:184
  73.4 11.2 %collective-permute-start.37 = (bf16[64,2048]{1,0:T(8,128)(2,1)S(1)}, bf16[64,2048]{1,0:T(8,128)(2,1)S(1)}, u32[]{:S(2)}, u32[]{:S(2)}) collective-permute-start(bf16[64,2048]{1,0:T(8,128)(2,1)S(1)} %get-tuple-element.74), channel_id=1, source_target_pairs={{0,8},{1,9},{2,10},{3,11},{4,12},{5,13},{6,14},{7,15},{8,0},{9,1},... | collective-permute-start | bytes 786440 | tf_op jit(solution)/shard_map/ppermute | solution.py:184
  84.6 7.0 %collective-permute-done.33.refs_0_ = bf16[64,2048]{1,0:T(8,128)(2,1)S(1)} collective-permute-done((bf16[64,2048]{1,0:T(8,128)(2,1)S(1)}, bf16[64,2048]{1,0:T(8,128)(2,1)S(1)}, u32[]{:S(2)}, u32[]{:S(2)}) %collective-permute-start.33) | collective-permute-done | bytes 262176 | tf_op jit(solution)/shard_map/ppermute | solution.py:184
  91.6 3.0 %collective-permute-done.37.refs_0_ = bf16[64,2048]{1,0:T(8,128)(2,1)S(1)} collective-permute-done((bf16[64,2048]{1,0:T(8,128)(2,1)S(1)}, bf16[64,2048]{1,0:T(8,128)(2,1)S(1)}, u32[]{:S(2)}, u32[]{:S(2)}) %collective-permute-start.37) | collective-permute-done | bytes 262176 | tf_op jit(solution)/shard_map/ppermute | solution.py:184
  96.0 10.6 %collective-permute-done.19.refs_1_ = bf16[128,2048]{1,0:T(8,128)(2,1)S(1)} collective-permute-done((bf16[128,2048]{1,0:T(8,128)(2,1)S(1)}, bf16[128,2048]{1,0:T(8,128)(2,1)S(1)}, u32[]{:S(2)}, u32[]{:S(2)}) %collective-permute-start.19) | collective-permute-done | bytes 524320 | tf_op jit(solution)/shard_map/ppermute | solution.py:184
  111.1 2.6 %shard_map.124 = bf16[128,2048]{1,0:T(8,128)(2,1)S(1)} custom-call(s32[1]{0:T(128)} %bitcast.index_ref, bf16[2,2048]{1,0:T(2,128)(2,1)S(1)} %bitcast.6, bf16[2048,256]{1,0:T(8,128)(2,1)S(1)} %get-tuple-element.64.up_a, bf16[2048,256]{1,0:T(8,128)(2,1)S(1)} %collective-permute-done.15.up_b, bf16[2048,512]{1,0:T(8,128)(2,1)S(1)} %get-tuple-element.65.in_a, ...), custom_call_target="tpu_custom_call" | custom-call | flops 1610612736 | bytes 13152260 | tf_op jit(solution)/shard_map/pallas_call | solution.py:195
  113.7 5.0 %collective-permute-done.22.refs_0_ = bf16[128,2048]{1,0:T(8,128)(2,1)S(1)} collective-permute-done((bf16[128,2048]{1,0:T(8,128)(2,1)S(1)}, bf16[128,2048]{1,0:T(8,128)(2,1)S(1)}, u32[]{:S(2)}, u32[]{:S(2)}) %collective-permute-start.22) | collective-permute-done | bytes 524320 | tf_op jit(solution)/shard_map/ppermute | solution.py:184
  118.7 2.6 %shard_map.125 = bf16[128,2048]{1,0:T(8,128)(2,1)S(1)} custom-call(s32[1]{0:T(128)} %bitcast.index_ref, bf16[2,2048]{1,0:T(2,128)(2,1)S(1)} %bitcast.7, bf16[2048,256]{1,0:T(8,128)(2,1)S(1)} %get-tuple-element.64.up_a, bf16[2048,256]{1,0:T(8,128)(2,1)S(1)} %collective-permute-done.15.up_b, bf16[2048,512]{1,0:T(8,128)(2,1)S(1)} %get-tuple-element.65.in_a, ...), custom_call_target="tpu_custom_call" | custom-call | flops 1610612736 | bytes 13152260 | tf_op jit(solution)/shard_map/pallas_call | solution.py:195
  121.4 2.1 %collective-permute-start.23 = (bf16[128,2048]{1,0:T(8,128)(2,1)S(1)}, bf16[128,2048]{1,0:T(8,128)(2,1)S(1)}, u32[]{:S(2)}, u32[]{:S(2)}) collective-permute-start(bf16[128,2048]{1,0:T(8,128)(2,1)S(1)} %shard_map.125), channel_id=1, source_target_pairs={{0,4},{1,5},{2,6},{3,7},{4,0},{5,1},{6,2},{7,3},{8,12},{9,13},{10,... | collective-permute-start | bytes 1572872 | tf_op jit(solution)/shard_map/ppermute | solution.py:184
  123.4 2.8 %shard_map.126 = (bf16[64,2048]{1,0:T(8,128)(2,1)S(1)}, bf16[64,2048]{1,0:T(8,128)(2,1)S(1)}) custom-call(s32[1]{0:T(128)} %bitcast.index_ref, bf16[2,2048]{1,0:T(2,128)(2,1)S(1)} %bitcast.8, bf16[2048,256]{1,0:T(8,128)(2,1)S(1)} %get-tuple-element.64.up_a, bf16[2048,256]{1,0:T(8,128)(2,1)S(1)} %collective-permute-done.15.up_b, ...), custom_call_target="tpu_custom_call" | custom-call | flops 1610612736 | bytes 13189124 | tf_op jit(solution)/shard_map/pallas_call | solution.py:195
  127.8 2.6 %shard_map.127 = (bf16[64,2048]{1,0:T(8,128)(2,1)S(1)}, bf16[64,2048]{1,0:T(8,128)(2,1)S(1)}) custom-call(s32[1]{0:T(128)} %bitcast.index_ref, bf16[2,2048]{1,0:T(2,128)(2,1)S(1)} %bitcast.9, bf16[2048,256]{1,0:T(8,128)(2,1)S(1)} %get-tuple-element.64.up_a, bf16[2048,256]{1,0:T(8,128)(2,1)S(1)} %collective-permute-done.15.up_b, ...), custom_call_target="tpu_custom_call" | custom-call | flops 1610612736 | bytes 13189124 | tf_op jit(solution)/shard_map/pallas_call | solution.py:195
  131.0 2.6 %shard_map.128 = (bf16[64,2048]{1,0:T(8,128)(2,1)S(1)}, bf16[64,2048]{1,0:T(8,128)(2,1)S(1)}) custom-call(s32[1]{0:T(128)} %bitcast.index_ref, bf16[2,2048]{1,0:T(2,128)(2,1)S(1)} %bitcast.10, bf16[2048,256]{1,0:T(8,128)(2,1)S(1)} %get-tuple-element.64.up_a, bf16[2048,256]{1,0:T(8,128)(2,1)S(1)} %collective-permute-done.15.up_b, ...), custom_call_target="tpu_custom_call" | custom-call | flops 1610612736 | bytes 13189124 | tf_op jit(solution)/shard_map/pallas_call | solution.py:195
  135.1 2.6 %shard_map.129 = (bf16[64,2048]{1,0:T(8,128)(2,1)S(1)}, bf16[64,2048]{1,0:T(8,128)(2,1)S(1)}) custom-call(s32[1]{0:T(128)} %bitcast.index_ref, bf16[2,2048]{1,0:T(2,128)(2,1)S(1)} %bitcast.11, bf16[2048,256]{1,0:T(8,128)(2,1)S(1)} %get-tuple-element.64.up_a, bf16[2048,256]{1,0:T(8,128)(2,1)S(1)} %collective-permute-done.15.up_b, ...), custom_call_target="tpu_custom_call" | custom-call | flops 1610612736 | bytes 13189124 | tf_op jit(solution)/shard_map/pallas_call | solution.py:195
  137.7 3.9 %shard_map.123 = (bf16[128,2048]{1,0:T(8,128)(2,1)S(1)}, bf16[128,2048]{1,0:T(8,128)(2,1)S(1)}) custom-call(s32[1]{0:T(128)} %bitcast.index_ref, bf16[2,2048]{1,0:T(2,128)(2,1)S(1)} %bitcast.12, bf16[2048,256]{1,0:T(8,128)(2,1)S(1)} %get-tuple-element.64.up_a, bf16[2048,256]{1,0:T(8,128)(2,1)S(1)} %collective-permute-done.15.up_b, ...), custom_call_target="tpu_custom_call" | custom-call | flops 3221225472 | bytes 13713412 | tf_op jit(solution)/shard_map/pallas_call | solution.py:195
  143.1 2.3 %collective-permute-start.39 = (bf16[64,2048]{1,0:T(8,128)(2,1)S(1)}, bf16[64,2048]{1,0:T(8,128)(2,1)S(1)}, u32[]{:S(2)}, u32[]{:S(2)}) collective-permute-start(bf16[64,2048]{1,0:T(8,128)(2,1)S(1)} %get-tuple-element.80), channel_id=1, source_target_pairs={{0,2},{1,3},{2,0},{3,1},{4,6},{5,7},{6,4},{7,5},{8,10},{9,11},{10,... | collective-permute-start | bytes 786440 | tf_op jit(solution)/shard_map/ppermute | solution.py:184
  148.0 3.2 %collective-permute-start.40 = (bf16[64,2048]{1,0:T(8,128)(2,1)S(1)}, bf16[64,2048]{1,0:T(8,128)(2,1)S(1)}, u32[]{:S(2)}, u32[]{:S(2)}) collective-permute-start(bf16[64,2048]{1,0:T(8,128)(2,1)S(1)} %add_convert_fusion.3), channel_id=1, source_target_pairs={{0,4},{1,5},{2,6},{3,7},{12,8},{13,9},{14,10},{15,11},{16,20},{17,... | collective-permute-start | bytes 786440 | tf_op jit(solution)/shard_map/ppermute | solution.py:184
  151.3 2.9 %collective-permute-start.28 = (bf16[64,2048]{1,0:T(8,128)(2,1)S(1)}, bf16[64,2048]{1,0:T(8,128)(2,1)S(1)}, u32[]{:S(2)}, u32[]{:S(2)}) collective-permute-start(bf16[64,2048]{1,0:T(8,128)(2,1)S(1)} %add_convert_fusion.4), channel_id=1, source_target_pairs={{0,12},{1,13},{2,14},{3,15},{4,8},{5,9},{6,10},{7,11},{8,4},{9,5},... | collective-permute-start | bytes 786440 | tf_op jit(solution)/shard_map/ppermute | solution.py:184
  154.5 3.4 %collective-permute-done.40 = bf16[64,2048]{1,0:T(8,128)(2,1)S(1)} collective-permute-done((bf16[64,2048]{1,0:T(8,128)(2,1)S(1)}, bf16[64,2048]{1,0:T(8,128)(2,1)S(1)}, u32[]{:S(2)}, u32[]{:S(2)}) %collective-permute-start.40) | collective-permute-done | bytes 262176 | tf_op jit(solution)/shard_map/ppermute | solution.py:184
  159.6 4.0 %collective-permute-done.28.refs_3_ = bf16[64,2048]{1,0:T(8,128)(2,1)S(1)} collective-permute-done((bf16[64,2048]{1,0:T(8,128)(2,1)S(1)}, bf16[64,2048]{1,0:T(8,128)(2,1)S(1)}, u32[]{:S(2)}, u32[]{:S(2)}) %collective-permute-start.28) | collective-permute-done | bytes 262176 | tf_op jit(solution)/shard_map/ppermute | solution.py:184
  163.6 12.3 %collective-permute-start.41 = (bf16[64,2048]{1,0:T(8,128)(2,1)S(1)}, bf16[64,2048]{1,0:T(8,128)(2,1)S(1)}, u32[]{:S(2)}, u32[]{:S(2)}) collective-permute-start(bf16[64,2048]{1,0:T(8,128)(2,1)S(1)} %add_convert_fusion.1), channel_id=1, source_target_pairs={{0,8},{1,9},{2,10},{3,11},{4,12},{5,13},{6,14},{7,15},{8,0},{9,1},... | collective-permute-start | bytes 786440 | tf_op jit(solution)/shard_map/ppermute | solution.py:184
  177.2 5.9 %collective-permute-done.41.refs_6_ = bf16[64,2048]{1,0:T(8,128)(2,1)S(1)} collective-permute-done((bf16[64,2048]{1,0:T(8,128)(2,1)S(1)}, bf16[64,2048]{1,0:T(8,128)(2,1)S(1)}, u32[]{:S(2)}, u32[]{:S(2)}) %collective-permute-start.41) | collective-permute-done | bytes 262176 | tf_op jit(solution)/shard_map/ppermute | solution.py:184
  (80 shorter events, 32.3 us)
Async XLA Ops:
  4.4 9.5 %collective-permute-start.1 = (bf16[128,384]{1,0:T(8,128)(2,1)S(1)}, bf16[128,384]{1,0:T(8,128)(2,1)S(1)}, u32[]{:S(2)}, u32[]{:S(2)}) collective-permute-start(bf16[128,384]{1,0:T(8,128)(2,1)S(1)} %get-tuple-element.47), channel_id=1, source_target_pairs={{0,4},{1,5},{2,6},{3,7},{4,0},{5,1},{6,2},{7,3},{8,12},{9,13},{10,... | collective-permute-start | bytes 294920 | tf_op jit(solution)/shard_map/ppermute | solution.py:184
  8.9 15.2 %collective-permute-start.4 = (bf16[128,384]{1,0:T(8,128)(2,1)S(1)}, bf16[128,384]{1,0:T(8,128)(2,1)S(1)}, u32[]{:S(2)}, u32[]{:S(2)}) collective-permute-start(bf16[128,384]{1,0:T(8,128)(2,1)S(1)} %get-tuple-element.50), channel_id=1, source_target_pairs={{0,10},{1,11},{2,8},{3,9},{4,14},{5,15},{6,12},{7,13},{8,2},{9,3},... | collective-permute-start | bytes 294920 | tf_op jit(solution)/shard_map/ppermute | solution.py:184
  10.2 13.9 %collective-permute-start.5 = (bf16[128,384]{1,0:T(8,128)(2,1)S(1)}, bf16[128,384]{1,0:T(8,128)(2,1)S(1)}, u32[]{:S(2)}, u32[]{:S(2)}) collective-permute-start(bf16[128,384]{1,0:T(8,128)(2,1)S(1)} %get-tuple-element.51), channel_id=1, source_target_pairs={{0,12},{1,13},{2,14},{3,15},{4,8},{5,9},{6,10},{7,11},{8,4},{9,5},... | collective-permute-start | bytes 294920 | tf_op jit(solution)/shard_map/ppermute | solution.py:184
  13.8 10.3 %collective-permute-start.6 = (bf16[128,384]{1,0:T(8,128)(2,1)S(1)}, bf16[128,384]{1,0:T(8,128)(2,1)S(1)}, u32[]{:S(2)}, u32[]{:S(2)}) collective-permute-start(bf16[128,384]{1,0:T(8,128)(2,1)S(1)} %get-tuple-element.52), channel_id=1, source_target_pairs={{0,14},{1,15},{2,12},{3,13},{4,10},{5,11},{6,8},{7,9},{8,6},{9,7},... | collective-permute-start | bytes 294920 | tf_op jit(solution)/shard_map/ppermute | solution.py:184
  24.3 84.7 %collective-permute-start.16 = (bf16[2048,512]{1,0:T(8,128)(2,1)}, bf16[2048,512]{1,0:T(8,128)(2,1)S(1)}, u32[]{:S(2)}, u32[]{:S(2)}) collective-permute-start(bf16[2048,512]{1,0:T(8,128)(2,1)} %bitcast.15), channel_id=1, source_target_pairs={{0,1},{1,0},{2,3},{3,2},{4,5},{5,4},{6,7},{7,6},{8,9},{9,8},{10,11... | collective-permute-start | bytes 6291464 | tf_op jit(solution)/shard_map/ppermute | solution.py:184
  24.8 86.3 %collective-permute-start.18 = (bf16[512,2048]{1,0:T(8,128)(2,1)}, bf16[512,2048]{1,0:T(8,128)(2,1)S(1)}, u32[]{:S(2)}, u32[]{:S(2)}) collective-permute-start(bf16[512,2048]{1,0:T(8,128)(2,1)} %bitcast.17), channel_id=1, source_target_pairs={{0,1},{1,0},{2,3},{3,2},{4,5},{5,4},{6,7},{7,6},{8,9},{9,8},{10,11... | collective-permute-start | bytes 6291464 | tf_op jit(solution)/shard_map/ppermute | solution.py:184
  39.3 9.7 %collective-permute-start.12 = (bf16[144,128]{1,0:T(8,128)(2,1)S(1)}, bf16[144,128]{1,0:T(8,128)(2,1)S(1)}, u32[]{:S(2)}, u32[]{:S(2)}) collective-permute-start(bf16[144,128]{1,0:T(8,128)(2,1)S(1)} %get-tuple-element.60), channel_id=1, source_target_pairs={{0,10},{1,11},{2,8},{3,9},{4,14},{5,15},{6,12},{7,13},{8,2},{9,3},... | collective-permute-start | bytes 110600 | tf_op jit(solution)/shard_map/ppermute | solution.py:184
  50.0 9.1 %collective-permute-start.25 = (bf16[64,2048]{1,0:T(8,128)(2,1)S(1)}, bf16[64,2048]{1,0:T(8,128)(2,1)S(1)}, u32[]{:S(2)}, u32[]{:S(2)}) collective-permute-start(bf16[64,2048]{1,0:T(8,128)(2,1)S(1)} %get-tuple-element.71), channel_id=1, source_target_pairs={{0,12},{1,13},{2,14},{3,15},{4,8},{5,9},{6,10},{7,11},{8,4},{9,5},... | collective-permute-start | bytes 786440 | tf_op jit(solution)/shard_map/ppermute | solution.py:184
  52.4 43.6 %collective-permute-start.15 = (bf16[2048,256]{1,0:T(8,128)(2,1)S(1)}, bf16[2048,256]{1,0:T(8,128)(2,1)S(1)}, u32[]{:S(2)}, u32[]{:S(2)}) collective-permute-start(bf16[2048,256]{1,0:T(8,128)(2,1)S(1)} %copy-done.3), channel_id=1, source_target_pairs={{0,1},{1,0},{2,3},{3,2},{4,5},{5,4},{6,7},{7,6},{8,9},{9,8},{10,11... | collective-permute-start | bytes 3145736 | tf_op jit(solution)/shard_map/ppermute | solution.py:184
  52.4 20.9 %collective-permute-start.29 = (bf16[64,2048]{1,0:T(8,128)(2,1)S(1)}, bf16[64,2048]{1,0:T(8,128)(2,1)S(1)}, u32[]{:S(2)}, u32[]{:S(2)}) collective-permute-start(bf16[64,2048]{1,0:T(8,128)(2,1)S(1)} %get-tuple-element.74), channel_id=1, source_target_pairs={{0,12},{1,13},{2,14},{3,15},{4,8},{5,9},{6,10},{7,11},{8,4},{9,5},... | collective-permute-start | bytes 786440 | tf_op jit(solution)/shard_map/ppermute | solution.py:184
  59.1 32.4 %collective-permute-start.33 = (bf16[64,2048]{1,0:T(8,128)(2,1)S(1)}, bf16[64,2048]{1,0:T(8,128)(2,1)S(1)}, u32[]{:S(2)}, u32[]{:S(2)}) collective-permute-start(bf16[64,2048]{1,0:T(8,128)(2,1)S(1)} %get-tuple-element.71), channel_id=1, source_target_pairs={{0,8},{1,9},{2,10},{3,11},{4,12},{5,13},{6,14},{7,15},{8,0},{9,1},... | collective-permute-start | bytes 786440 | tf_op jit(solution)/shard_map/ppermute | solution.py:184
  73.4 21.2 %collective-permute-start.37 = (bf16[64,2048]{1,0:T(8,128)(2,1)S(1)}, bf16[64,2048]{1,0:T(8,128)(2,1)S(1)}, u32[]{:S(2)}, u32[]{:S(2)}) collective-permute-start(bf16[64,2048]{1,0:T(8,128)(2,1)S(1)} %get-tuple-element.74), channel_id=1, source_target_pairs={{0,8},{1,9},{2,10},{3,11},{4,12},{5,13},{6,14},{7,15},{8,0},{9,1},... | collective-permute-start | bytes 786440 | tf_op jit(solution)/shard_map/ppermute | solution.py:184
  91.6 15.1 %collective-permute-start.17 = (bf16[2048,256]{1,0:T(8,128)(2,1)S(1)}, bf16[2048,256]{1,0:T(8,128)(2,1)S(1)}, u32[]{:S(2)}, u32[]{:S(2)}) collective-permute-start(bf16[2048,256]{1,0:T(8,128)(2,1)S(1)} %copy-done.4), channel_id=1, source_target_pairs={{0,1},{1,0},{2,3},{3,2},{4,5},{5,4},{6,7},{7,6},{8,9},{9,8},{10,11... | collective-permute-start | bytes 3145736 | tf_op jit(solution)/shard_map/ppermute | solution.py:184
  94.6 12.1 %collective-permute-start.19 = (bf16[128,2048]{1,0:T(8,128)(2,1)S(1)}, bf16[128,2048]{1,0:T(8,128)(2,1)S(1)}, u32[]{:S(2)}, u32[]{:S(2)}) collective-permute-start(bf16[128,2048]{1,0:T(8,128)(2,1)S(1)} %get-tuple-element.68.refs_0_), channel_id=1, source_target_pairs={{0,2},{1,3},{2,0},{3,1},{4,6},{5,7},{6,4},{7,5},{8,10},{9,11},{10,... | collective-permute-start | bytes 1572872 | tf_op jit(solution)/shard_map/ppermute | solution.py:184
  96.0 13.0 %collective-permute-start.20 = (bf16[128,2048]{1,0:T(8,128)(2,1)S(1)}, bf16[128,2048]{1,0:T(8,128)(2,1)S(1)}, u32[]{:S(2)}, u32[]{:S(2)}) collective-permute-start(bf16[128,2048]{1,0:T(8,128)(2,1)S(1)} %get-tuple-element.68.refs_0_), channel_id=1, source_target_pairs={{0,4},{1,5},{2,6},{3,7},{4,0},{5,1},{6,2},{7,3},{8,12},{9,13},{10,... | collective-permute-start | bytes 1572872 | tf_op jit(solution)/shard_map/ppermute | solution.py:184
  106.7 12.1 %collective-permute-start.22 = (bf16[128,2048]{1,0:T(8,128)(2,1)S(1)}, bf16[128,2048]{1,0:T(8,128)(2,1)S(1)}, u32[]{:S(2)}, u32[]{:S(2)}) collective-permute-start(bf16[128,2048]{1,0:T(8,128)(2,1)S(1)} %collective-permute-done.19.refs_1_), channel_id=1, source_target_pairs={{0,4},{1,5},{2,6},{3,7},{4,0},{5,1},{6,2},{7,3},{8,12},{9,13},{10,... | collective-permute-start | bytes 1572872 | tf_op jit(solution)/shard_map/ppermute | solution.py:184
  106.7 14.7 %collective-permute-start.26 = (bf16[64,2048]{1,0:T(8,128)(2,1)S(1)}, bf16[64,2048]{1,0:T(8,128)(2,1)S(1)}, u32[]{:S(2)}, u32[]{:S(2)}) collective-permute-start(bf16[64,2048]{1,0:T(8,128)(2,1)S(1)} %collective-permute-done.25.refs_0_), channel_id=1, source_target_pairs={{0,2},{1,3},{2,0},{3,1},{4,6},{5,7},{6,4},{7,5},{8,10},{9,11},{10,... | collective-permute-start | bytes 786440 | tf_op jit(solution)/shard_map/ppermute | solution.py:184
  109.0 17.2 %collective-permute-start.30 = (bf16[64,2048]{1,0:T(8,128)(2,1)S(1)}, bf16[64,2048]{1,0:T(8,128)(2,1)S(1)}, u32[]{:S(2)}, u32[]{:S(2)}) collective-permute-start(bf16[64,2048]{1,0:T(8,128)(2,1)S(1)} %collective-permute-done.29.refs_0_), channel_id=1, source_target_pairs={{0,2},{1,3},{2,0},{3,1},{4,6},{5,7},{6,4},{7,5},{8,10},{9,11},{10,... | collective-permute-start | bytes 786440 | tf_op jit(solution)/shard_map/ppermute | solution.py:184
  109.0 21.3 %collective-permute-start.34 = (bf16[64,2048]{1,0:T(8,128)(2,1)S(1)}, bf16[64,2048]{1,0:T(8,128)(2,1)S(1)}, u32[]{:S(2)}, u32[]{:S(2)}) collective-permute-start(bf16[64,2048]{1,0:T(8,128)(2,1)S(1)} %collective-permute-done.33.refs_0_), channel_id=1, source_target_pairs={{0,2},{1,3},{2,0},{3,1},{4,6},{5,7},{6,4},{7,5},{8,10},{9,11},{10,... | collective-permute-start | bytes 786440 | tf_op jit(solution)/shard_map/ppermute | solution.py:184
  111.1 22.5 %collective-permute-start.38 = (bf16[64,2048]{1,0:T(8,128)(2,1)S(1)}, bf16[64,2048]{1,0:T(8,128)(2,1)S(1)}, u32[]{:S(2)}, u32[]{:S(2)}) collective-permute-start(bf16[64,2048]{1,0:T(8,128)(2,1)S(1)} %collective-permute-done.37.refs_0_), channel_id=1, source_target_pairs={{0,2},{1,3},{2,0},{3,1},{4,6},{5,7},{6,4},{7,5},{8,10},{9,11},{10,... | collective-permute-start | bytes 786440 | tf_op jit(solution)/shard_map/ppermute | solution.py:184
  118.7 58.4 %collective-permute-start.21 = (bf16[128,2048]{1,0:T(8,128)(2,1)S(1)}, bf16[128,2048]{1,0:T(8,128)(2,1)S(1)}, u32[]{:S(2)}, u32[]{:S(2)}) collective-permute-start(bf16[128,2048]{1,0:T(8,128)(2,1)S(1)} %shard_map.124), channel_id=1, source_target_pairs={{0,4},{1,5},{2,6},{3,7},{4,0},{5,1},{6,2},{7,3},{8,12},{9,13},{10,... | collective-permute-start | bytes 1572872 | tf_op jit(solution)/shard_map/ppermute | solution.py:184
  121.4 30.0 %collective-permute-start.23 = (bf16[128,2048]{1,0:T(8,128)(2,1)S(1)}, bf16[128,2048]{1,0:T(8,128)(2,1)S(1)}, u32[]{:S(2)}, u32[]{:S(2)}) collective-permute-start(bf16[128,2048]{1,0:T(8,128)(2,1)S(1)} %shard_map.125), channel_id=1, source_target_pairs={{0,4},{1,5},{2,6},{3,7},{4,0},{5,1},{6,2},{7,3},{8,12},{9,13},{10,... | collective-permute-start | bytes 1572872 | tf_op jit(solution)/shard_map/ppermute | solution.py:184
  126.2 19.2 %collective-permute-start.27 = (bf16[64,2048]{1,0:T(8,128)(2,1)S(1)}, bf16[64,2048]{1,0:T(8,128)(2,1)S(1)}, u32[]{:S(2)}, u32[]{:S(2)}) collective-permute-start(bf16[64,2048]{1,0:T(8,128)(2,1)S(1)} %get-tuple-element.73), channel_id=1, source_target_pairs={{0,2},{1,3},{2,0},{3,1},{4,6},{5,7},{6,4},{7,5},{8,10},{9,11},{10,... | collective-permute-start | bytes 786440 | tf_op jit(solution)/shard_map/ppermute | solution.py:184
  130.3 12.8 %collective-permute-start.31 = (bf16[64,2048]{1,0:T(8,128)(2,1)S(1)}, bf16[64,2048]{1,0:T(8,128)(2,1)S(1)}, u32[]{:S(2)}, u32[]{:S(2)}) collective-permute-start(bf16[64,2048]{1,0:T(8,128)(2,1)S(1)} %get-tuple-element.76), channel_id=1, source_target_pairs={{0,2},{1,3},{2,0},{3,1},{4,6},{5,7},{6,4},{7,5},{8,10},{9,11},{10,... | collective-permute-start | bytes 786440 | tf_op jit(solution)/shard_map/ppermute | solution.py:184
  133.6 14.5 %collective-permute-start.35 = (bf16[64,2048]{1,0:T(8,128)(2,1)S(1)}, bf16[64,2048]{1,0:T(8,128)(2,1)S(1)}, u32[]{:S(2)}, u32[]{:S(2)}) collective-permute-start(bf16[64,2048]{1,0:T(8,128)(2,1)S(1)} %get-tuple-element.78), channel_id=1, source_target_pairs={{0,2},{1,3},{2,0},{3,1},{4,6},{5,7},{6,4},{7,5},{8,10},{9,11},{10,... | collective-permute-start | bytes 786440 | tf_op jit(solution)/shard_map/ppermute | solution.py:184
  143.1 11.3 %collective-permute-start.39 = (bf16[64,2048]{1,0:T(8,128)(2,1)S(1)}, bf16[64,2048]{1,0:T(8,128)(2,1)S(1)}, u32[]{:S(2)}, u32[]{:S(2)}) collective-permute-start(bf16[64,2048]{1,0:T(8,128)(2,1)S(1)} %get-tuple-element.80), channel_id=1, source_target_pairs={{0,2},{1,3},{2,0},{3,1},{4,6},{5,7},{6,4},{7,5},{8,10},{9,11},{10,... | collective-permute-start | bytes 786440 | tf_op jit(solution)/shard_map/ppermute | solution.py:184
  145.5 30.4 %collective-permute-start.32 = (bf16[64,2048]{1,0:T(8,128)(2,1)S(1)}, bf16[64,2048]{1,0:T(8,128)(2,1)S(1)}, u32[]{:S(2)}, u32[]{:S(2)}) collective-permute-start(bf16[64,2048]{1,0:T(8,128)(2,1)S(1)} %add_convert_fusion.3), channel_id=1, source_target_pairs={{4,8},{5,9},{6,10},{7,11},{8,4},{9,5},{10,6},{11,7},{20,24},{21,25... | collective-permute-start | bytes 786440 | tf_op jit(solution)/shard_map/ppermute | solution.py:184
  148.0 9.9 %collective-permute-start.40 = (bf16[64,2048]{1,0:T(8,128)(2,1)S(1)}, bf16[64,2048]{1,0:T(8,128)(2,1)S(1)}, u32[]{:S(2)}, u32[]{:S(2)}) collective-permute-start(bf16[64,2048]{1,0:T(8,128)(2,1)S(1)} %add_convert_fusion.3), channel_id=1, source_target_pairs={{0,4},{1,5},{2,6},{3,7},{12,8},{13,9},{14,10},{15,11},{16,20},{17,... | collective-permute-start | bytes 786440 | tf_op jit(solution)/shard_map/ppermute | solution.py:184
  151.3 12.3 %collective-permute-start.28 = (bf16[64,2048]{1,0:T(8,128)(2,1)S(1)}, bf16[64,2048]{1,0:T(8,128)(2,1)S(1)}, u32[]{:S(2)}, u32[]{:S(2)}) collective-permute-start(bf16[64,2048]{1,0:T(8,128)(2,1)S(1)} %add_convert_fusion.4), channel_id=1, source_target_pairs={{0,12},{1,13},{2,14},{3,15},{4,8},{5,9},{6,10},{7,11},{8,4},{9,5},... | collective-permute-start | bytes 786440 | tf_op jit(solution)/shard_map/ppermute | solution.py:184
  154.4 22.8 %collective-permute-start.36 = (bf16[64,2048]{1,0:T(8,128)(2,1)S(1)}, bf16[64,2048]{1,0:T(8,128)(2,1)S(1)}, u32[]{:S(2)}, u32[]{:S(2)}) collective-permute-start(bf16[64,2048]{1,0:T(8,128)(2,1)S(1)} %add_convert_fusion.2), channel_id=1, source_target_pairs={{0,8},{1,9},{2,10},{3,11},{4,12},{5,13},{6,14},{7,15},{8,0},{9,1},... | collective-permute-start | bytes 786440 | tf_op jit(solution)/shard_map/ppermute | solution.py:184
  157.9 25.1 %collective-permute-start.24 = (bf16[128,2048]{1,0:T(8,128)(2,1)S(1)}, bf16[128,2048]{1,0:T(8,128)(2,1)S(1)}, u32[]{:S(2)}, u32[]{:S(2)}) collective-permute-start(bf16[128,2048]{1,0:T(8,128)(2,1)S(1)} %add_convert_fusion), channel_id=1, source_target_pairs={{0,2},{1,3},{2,0},{3,1},{4,6},{5,7},{6,4},{7,5},{8,10},{9,11},{10,... | collective-permute-start | bytes 1572872 | tf_op jit(solution)/shard_map/ppermute | solution.py:184
  163.6 19.4 %collective-permute-start.41 = (bf16[64,2048]{1,0:T(8,128)(2,1)S(1)}, bf16[64,2048]{1,0:T(8,128)(2,1)S(1)}, u32[]{:S(2)}, u32[]{:S(2)}) collective-permute-start(bf16[64,2048]{1,0:T(8,128)(2,1)S(1)} %add_convert_fusion.1), channel_id=1, source_target_pairs={{0,8},{1,9},{2,10},{3,11},{4,12},{5,13},{6,14},{7,15},{8,0},{9,1},... | collective-permute-start | bytes 786440 | tf_op jit(solution)/shard_map/ppermute | solution.py:184
  (15 other events, 183.4 us)
